TPU v7x, 1024 devices: a whole 8x8x8 slice. The times are simulated.
1024 devices in a mesh: batch: 32 (over x_lo, z, core), mem: 32 (over x_hi, y).
Axes of the slice: x: 8 (x_hi: 4, x_lo: 2; x = x_hi * 2 + x_lo), y: 8, z: 8, core: 2. Of those that a mesh axis runs over, the one named last changes fastest.
Arguments:
- queries: bfloat16 [131072, 256], P(('mem', 'batch')), may hold values from -10 to 10
- positives: bfloat16 [131072, 256], P(('mem', 'batch')), may hold values from -0.25 to 0.25, as said below
- pos_ids: int32 [131072], replicated, may hold values from 0 to 31
- pos_logq: int32 [131072], replicated, may hold values from -10240 to -4097
- mem_items: bfloat16 [32768, 256], P(('batch', 'mem')), may hold values from -0.375 to 0.375
- mem_ids: int32 [32768], replicated, may hold values from 0 to 31
- mem_logq: int32 [32768], replicated, may hold values from -12288 to -6145
- mem_age: int32 [32768], replicated, may hold values from 0 to 23
- counts: int32 [16384], replicated, may hold values from 1 to 64, 131072 in all
Outputs:
- row_loss: float32 [131072], P(('mem', 'batch'))
- query_grad: float32 [131072, 256], P(('mem', 'batch'))
- positive_grad: float32 [131072, 256], P(('mem', 'batch'))
Inputs may be any that keep to these rules, and one draw needn't show every extreme that they name: `positives`: item embeddings. The counts sum to 131072; the largest is 64.
All inputs are finite; a program needn't handle non-finite values.
Results may differ from a plain program's by a relative error of at most 0.0033.
Values may be sent and summed in bfloat16 or wider, within the bound.
A program may use at most 32 MiB of HBM per device.

v0:
```python
import jax
import jax.numpy as jnp
from jax import lax
from jax.sharding import PartitionSpec as P

AGE_LIMIT = 16


inv_temp = 8.0
logq_unit = 1.0 / 1024.0
very_low = -1e30


def request_of(counts, positions):
    req_ends = jnp.cumsum(counts)
    return jnp.searchsorted(req_ends, positions, side="right")


def scores(left_mat, right_mat):
    return lax.dot_general(
        left_mat, right_mat, (((1,), (1,)), ((), ())), preferred_element_type=jnp.float32
    )


def transposed(left_mat, right_mat):
    return lax.dot_general(
        left_mat, right_mat, (((0,), (0,)), ((), ())), preferred_element_type=jnp.float32
    )


def masked_exp(tile_logits, level):
    return jnp.where(tile_logits > very_low, jnp.exp(tile_logits - level[:, None]), 0.0)


def body(queries, positives, pos_ids, pos_logq, mem_items, mem_ids, mem_logq, mem_age, counts):
    own_count = queries.shape[0]
    batch_count = lax.axis_size("batch")
    group_rows = own_count * batch_count
    bank_rows = mem_items.shape[0] * lax.axis_size("mem")
    batch_index = lax.axis_index("batch")
    group_first = lax.axis_index("mem") * group_rows
    own_first = group_first + batch_index * own_count
    bank_first = batch_index * bank_rows
    own_rows = own_first + jnp.arange(own_count, dtype=jnp.int32)
    own_req = request_of(counts, own_rows)
    weight = 1.0 / jnp.take(counts, own_req).astype(jnp.float32)
    own_ids = lax.dynamic_slice_in_dim(pos_ids, own_first, own_count, 0)
    own_shift = (
        -lax.dynamic_slice_in_dim(pos_logq, own_first, own_count, 0).astype(jnp.float32) * logq_unit
    )
    cand_rows = group_first + jnp.arange(group_rows, dtype=jnp.int32)
    cand_req = request_of(counts, cand_rows)
    cand_ids = lax.dynamic_slice_in_dim(pos_ids, group_first, group_rows, 0)
    cand_shift = (
        -lax.dynamic_slice_in_dim(pos_logq, group_first, group_rows, 0).astype(jnp.float32)
        * logq_unit
    )
    bank_ids = lax.dynamic_slice_in_dim(mem_ids, bank_first, bank_rows, 0)
    bank_shift = (
        -lax.dynamic_slice_in_dim(mem_logq, bank_first, bank_rows, 0).astype(jnp.float32)
        * logq_unit
    )
    bank_live = lax.dynamic_slice_in_dim(mem_age, bank_first, bank_rows, 0) < AGE_LIMIT
    bank_items = lax.all_gather(mem_items, "mem", axis=0, tiled=True)
    mem_mask = bank_live[None, :] & (bank_ids[None, :] != own_ids[:, None])
    mem_logits = jnp.where(
        mem_mask, inv_temp * scores(queries, bank_items) + bank_shift[None, :], very_low
    )
    mem_max = jnp.max(mem_logits, axis=1)
    group_items = lax.all_gather(positives, "batch", axis=0, tiled=True)
    piece_rows = group_items.shape[0]
    col_rows = group_first + jnp.arange(piece_rows, dtype=jnp.int32)
    kept_mask = (col_rows[None, :] == own_rows[:, None]) | (
        cand_ids[None, :] != own_ids[:, None]
    ) & (cand_req[None, :] != own_req[:, None])
    group_logits = jnp.where(
        kept_mask, inv_temp * scores(queries, group_items) + cand_shift[None, :], very_low
    )
    row_max = jnp.maximum(jnp.max(group_logits, axis=1), mem_max)
    pos_total = jnp.sum(masked_exp(group_logits, row_max), axis=1)
    mem_total = jnp.sum(masked_exp(mem_logits, row_max), axis=1)
    row_lse = row_max + jnp.log(pos_total + mem_total)
    pos_coef = (weight[:, None] * masked_exp(group_logits, row_lse)).astype(jnp.bfloat16)
    mem_coef = (weight[:, None] * masked_exp(mem_logits, row_lse)).astype(jnp.bfloat16)
    own_term = inv_temp * weight[:, None]
    query_grad = inv_temp * (
        jnp.dot(pos_coef, group_items, preferred_element_type=jnp.float32)
        + jnp.dot(mem_coef, bank_items, preferred_element_type=jnp.float32)
    ) - own_term * positives.astype(jnp.float32)
    column_share = lax.psum_scatter(
        inv_temp * transposed(pos_coef, queries), "batch", scatter_dimension=0, tiled=True
    )
    positive_grad = column_share - own_term * queries.astype(jnp.float32)
    own_logit = (
        inv_temp * jnp.sum(queries.astype(jnp.float32) * positives.astype(jnp.float32), axis=1)
        + own_shift
    )
    return (row_lse - own_logit, query_grad, positive_grad)


def solution(mesh):
    in_specs = (
        P(("mem", "batch"), None),
        P(("mem", "batch"), None),
        P(),
        P(),
        P(("batch", "mem"), None),
        P(),
        P(),
        P(),
        P(),
    )
    out_specs = (P(("mem", "batch")), P(("mem", "batch"), None), P(("mem", "batch"), None))
    return jax.shard_map(body, mesh=mesh, in_specs=in_specs, out_specs=out_specs, check_vma=False)
```

profile of v0, /device:TPU:1, one launch (start us, length us, event | category | flops | bytes accessed | tf_op | source)
XLA Modules:
  0.0 612.5 jit_solution(7531723254533697450)
XLA Ops:
  9.6 346.9 %while.48 = (s32[]{:T(128)}, u32[4096]{0:T(1024)S(1)}, u32[4096]{0:T(1024)S(1)}, s32[16384]{0:T(1024)S(1)}, s32[]{:T(128)}, /*index=5*/s32[]{:T(128)}, s32[]{:T(128)}, s32[]{}) while((s32[]{:T(128)}, u32[4096]{0:T(1024)S(1)}, u32[4096]{0:T(1024)S(1)}, s32[16384]{0:T(1024)S(1)}, s32[]{:T(128)}, /*index=5*/s32[]{:T(128)}, s32[]{:T(128)}, ...), condition=%wide.region_3.4_spmd.clone, body=%wide.region_2.3_spmd.clone.sunk | while | flops 81924 | bytes 254065 | solution.py:16
  9.7 23.0 %gather_fusion = s32[4096]{0:T(1024)S(1)} fusion(s32[16384]{0:T(1024)S(1)} %get-tuple-element.322, u32[4096]{0:T(1024)S(1)} %broadcast_clamp_fusion.2), kind=kCustom, calls=%fused_computation.clone.clone.1 | custom fusion | bytes 49152 | tf_op jit(solution)/shard_map/jit(searchsorted)/jit(_searchsorted_scan_impl)/vmap(jit(_searchsorted_scan_impl))/while/body/eval_jaxpr/gather | solution.py:16
  32.8 23.0 %gather_fusion = s32[4096]{0:T(1024)S(1)} fusion(s32[16384]{0:T(1024)S(1)} %get-tuple-element.322, u32[4096]{0:T(1024)S(1)} %broadcast_clamp_fusion.2), kind=kCustom, calls=%fused_computation.clone.clone.1 | custom fusion | bytes 49152 | tf_op jit(solution)/shard_map/jit(searchsorted)/jit(_searchsorted_scan_impl)/vmap(jit(_searchsorted_scan_impl))/while/body/eval_jaxpr/gather | solution.py:16
  55.9 23.0 %gather_fusion = s32[4096]{0:T(1024)S(1)} fusion(s32[16384]{0:T(1024)S(1)} %get-tuple-element.322, u32[4096]{0:T(1024)S(1)} %broadcast_clamp_fusion.2), kind=kCustom, calls=%fused_computation.clone.clone.1 | custom fusion | bytes 49152 | tf_op jit(solution)/shard_map/jit(searchsorted)/jit(_searchsorted_scan_impl)/vmap(jit(_searchsorted_scan_impl))/while/body/eval_jaxpr/gather | solution.py:16
  79.1 23.0 %gather_fusion = s32[4096]{0:T(1024)S(1)} fusion(s32[16384]{0:T(1024)S(1)} %get-tuple-element.322, u32[4096]{0:T(1024)S(1)} %broadcast_clamp_fusion.2), kind=kCustom, calls=%fused_computation.clone.clone.1 | custom fusion | bytes 49152 | tf_op jit(solution)/shard_map/jit(searchsorted)/jit(_searchsorted_scan_impl)/vmap(jit(_searchsorted_scan_impl))/while/body/eval_jaxpr/gather | solution.py:16
  102.2 23.0 %gather_fusion = s32[4096]{0:T(1024)S(1)} fusion(s32[16384]{0:T(1024)S(1)} %get-tuple-element.322, u32[4096]{0:T(1024)S(1)} %broadcast_clamp_fusion.2), kind=kCustom, calls=%fused_computation.clone.clone.1 | custom fusion | bytes 49152 | tf_op jit(solution)/shard_map/jit(searchsorted)/jit(_searchsorted_scan_impl)/vmap(jit(_searchsorted_scan_impl))/while/body/eval_jaxpr/gather | solution.py:16
  125.3 23.0 %gather_fusion = s32[4096]{0:T(1024)S(1)} fusion(s32[16384]{0:T(1024)S(1)} %get-tuple-element.322, u32[4096]{0:T(1024)S(1)} %broadcast_clamp_fusion.2), kind=kCustom, calls=%fused_computation.clone.clone.1 | custom fusion | bytes 49152 | tf_op jit(solution)/shard_map/jit(searchsorted)/jit(_searchsorted_scan_impl)/vmap(jit(_searchsorted_scan_impl))/while/body/eval_jaxpr/gather | solution.py:16
  148.4 23.0 %gather_fusion = s32[4096]{0:T(1024)S(1)} fusion(s32[16384]{0:T(1024)S(1)} %get-tuple-element.322, u32[4096]{0:T(1024)S(1)} %broadcast_clamp_fusion.2), kind=kCustom, calls=%fused_computation.clone.clone.1 | custom fusion | bytes 49152 | tf_op jit(solution)/shard_map/jit(searchsorted)/jit(_searchsorted_scan_impl)/vmap(jit(_searchsorted_scan_impl))/while/body/eval_jaxpr/gather | solution.py:16
  171.6 23.0 %gather_fusion = s32[4096]{0:T(1024)S(1)} fusion(s32[16384]{0:T(1024)S(1)} %get-tuple-element.322, u32[4096]{0:T(1024)S(1)} %broadcast_clamp_fusion.2), kind=kCustom, calls=%fused_computation.clone.clone.1 | custom fusion | bytes 49152 | tf_op jit(solution)/shard_map/jit(searchsorted)/jit(_searchsorted_scan_impl)/vmap(jit(_searchsorted_scan_impl))/while/body/eval_jaxpr/gather | solution.py:16
  194.7 23.0 %gather_fusion = s32[4096]{0:T(1024)S(1)} fusion(s32[16384]{0:T(1024)S(1)} %get-tuple-element.322, u32[4096]{0:T(1024)S(1)} %broadcast_clamp_fusion.2), kind=kCustom, calls=%fused_computation.clone.clone.1 | custom fusion | bytes 49152 | tf_op jit(solution)/shard_map/jit(searchsorted)/jit(_searchsorted_scan_impl)/vmap(jit(_searchsorted_scan_impl))/while/body/eval_jaxpr/gather | solution.py:16
  217.8 23.0 %gather_fusion = s32[4096]{0:T(1024)S(1)} fusion(s32[16384]{0:T(1024)S(1)} %get-tuple-element.322, u32[4096]{0:T(1024)S(1)} %broadcast_clamp_fusion.2), kind=kCustom, calls=%fused_computation.clone.clone.1 | custom fusion | bytes 49152 | tf_op jit(solution)/shard_map/jit(searchsorted)/jit(_searchsorted_scan_impl)/vmap(jit(_searchsorted_scan_impl))/while/body/eval_jaxpr/gather | solution.py:16
  241.0 23.0 %gather_fusion = s32[4096]{0:T(1024)S(1)} fusion(s32[16384]{0:T(1024)S(1)} %get-tuple-element.322, u32[4096]{0:T(1024)S(1)} %broadcast_clamp_fusion.2), kind=kCustom, calls=%fused_computation.clone.clone.1 | custom fusion | bytes 49152 | tf_op jit(solution)/shard_map/jit(searchsorted)/jit(_searchsorted_scan_impl)/vmap(jit(_searchsorted_scan_impl))/while/body/eval_jaxpr/gather | solution.py:16
  264.1 23.0 %gather_fusion = s32[4096]{0:T(1024)S(1)} fusion(s32[16384]{0:T(1024)S(1)} %get-tuple-element.322, u32[4096]{0:T(1024)S(1)} %broadcast_clamp_fusion.2), kind=kCustom, calls=%fused_computation.clone.clone.1 | custom fusion | bytes 49152 | tf_op jit(solution)/shard_map/jit(searchsorted)/jit(_searchsorted_scan_impl)/vmap(jit(_searchsorted_scan_impl))/while/body/eval_jaxpr/gather | solution.py:16
  287.2 23.0 %gather_fusion = s32[4096]{0:T(1024)S(1)} fusion(s32[16384]{0:T(1024)S(1)} %get-tuple-element.322, u32[4096]{0:T(1024)S(1)} %broadcast_clamp_fusion.2), kind=kCustom, calls=%fused_computation.clone.clone.1 | custom fusion | bytes 49152 | tf_op jit(solution)/shard_map/jit(searchsorted)/jit(_searchsorted_scan_impl)/vmap(jit(_searchsorted_scan_impl))/while/body/eval_jaxpr/gather | solution.py:16
  310.3 23.0 %gather_fusion = s32[4096]{0:T(1024)S(1)} fusion(s32[16384]{0:T(1024)S(1)} %get-tuple-element.322, u32[4096]{0:T(1024)S(1)} %broadcast_clamp_fusion.2), kind=kCustom, calls=%fused_computation.clone.clone.1 | custom fusion | bytes 49152 | tf_op jit(solution)/shard_map/jit(searchsorted)/jit(_searchsorted_scan_impl)/vmap(jit(_searchsorted_scan_impl))/while/body/eval_jaxpr/gather | solution.py:16
  333.5 23.0 %gather_fusion = s32[4096]{0:T(1024)S(1)} fusion(s32[16384]{0:T(1024)S(1)} %get-tuple-element.322, u32[4096]{0:T(1024)S(1)} %broadcast_clamp_fusion.2), kind=kCustom, calls=%fused_computation.clone.clone.1 | custom fusion | bytes 49152 | tf_op jit(solution)/shard_map/jit(searchsorted)/jit(_searchsorted_scan_impl)/vmap(jit(_searchsorted_scan_impl))/while/body/eval_jaxpr/gather | solution.py:16
  356.6 18.3 %while.49 = (s32[]{:T(128)}, u32[128]{0:T(128)S(1)}, u32[128]{0:T(128)S(1)}, s32[16384]{0:T(1024)S(1)}, s32[]{:T(128)}, /*index=5*/s32[]{:T(128)}, s32[]{:T(128)}, s32[]{}) while((s32[]{:T(128)}, u32[128]{0:T(128)S(1)}, u32[128]{0:T(128)S(1)}, s32[16384]{0:T(1024)S(1)}, s32[]{:T(128)}, /*index=5*/s32[]{:T(128)}, s32[]{:T(128)}, ...), condition=%wide.region_5.6_spmd.clone, body=%wide.region_4.5_spmd.clone.sunk | while | flops 2820 | bytes 10352 | solution.py:16
  379.1 73.6 %all_gather.7 = bf16[1024,256]{1,0:T(8,128)(2,1)S(1)} all-gather(bf16[32,256]{1,0:T(8,128)(2,1)S(1)} %copy-done.8), channel_id=1, replica_groups=mesh['batch'=32,'mem'=32] {'mem'}, dimensions={0}, use_global_device_ids=true | all-gather | bytes 540672 | tf_op jit(solution)/shard_map/all_gather | solution.py:64
  454.0 2.8 fusion.19
  457.6 1.3 add_subtract_fusion
  459.4 2.7 convolution_multiply_fusion
  462.1 1.6 copy-done.1
  465.8 138.2 %reduce-scatter.2.cloned.1.call-done = f32[128,256]{1,0:T(8,128)} async-done(((f32[4096,256]{1,0:T(8,128)}), f32[128,256]{1,0:T(8,128)}) %reduce-scatter.2.cloned.1.call-update) | async-done | bytes 131088 | tf_op jit(solution)/shard_map/reduce_scatter | solution.py:90
  604.0 1.6 fusion.15
  (179 shorter events, 29.6 us)
Async XLA Ops:
  7.2 446.8 %all-gather.2.cloned.1.call-start = ((), (), s32[]{:S(2)}) async-start(), calls=%async_computation.1 | async-start | bytes 2162688 | tf_op jit(solution)/shard_map/all_gather | solution.py:70
  7.9 596.1 %reduce-scatter.2.cloned.1.call-start = ((), (), s32[]{:S(2)}) async-start(), calls=%async_computation.2 | async-start | bytes 4325376 | tf_op jit(solution)/shard_map/reduce_scatter | solution.py:90
  9.6 365.3 %copy-start.9 = (s32[131072]{0:T(1024)S(1)}, s32[131072]{0:T(1024)}, u32[]{:S(2)}) copy-start(s32[131072]{0:T(1024)} %param.15) | copy-start | bytes 1572868
  356.6 18.5 %copy-start = (s32[16384]{0:T(1024)S(1)}, s32[16384]{0:T(1024)}, u32[]{:S(2)}) copy-start(s32[16384]{0:T(1024)} %param.21) | copy-start | bytes 196612
  356.6 22.4 %copy-start.2 = (bf16[128,256]{1,0:T(8,128)(2,1)S(1)}, bf16[128,256]{1,0:T(8,128)(2,1)}, u32[]{:S(2)}) copy-start(bf16[128,256]{1,0:T(8,128)(2,1)} %param.13) | copy-start | bytes 196612
  356.6 22.4 %copy-start.7 = (bf16[128,256]{1,0:T(8,128)(2,1)S(1)}, bf16[128,256]{1,0:T(8,128)(2,1)}, u32[]{:S(2)}) copy-start(bf16[128,256]{1,0:T(8,128)(2,1)} %param.14) | copy-start | bytes 196612
  356.6 22.5 %copy-start.8 = (bf16[32,256]{1,0:T(8,128)(2,1)S(1)}, bf16[32,256]{1,0:T(8,128)(2,1)}, u32[]{:S(2)}) copy-start(bf16[32,256]{1,0:T(8,128)(2,1)} %param.17) | copy-start | bytes 49156
  374.9 79.1 %dynamic-slice-start = ((s32[131072]{0:T(1024)}, s32[]{:T(128)}), s32[4096]{0:T(1024)S(1)}, s32[]{:S(2)}) async-start(s32[131072]{0:T(1024)} %param.15, s32[]{:T(128)} %select_n.69), calls=%async_computation.3 | async-start | bytes 33280 | tf_op jit(solution)/shard_map/dynamic_slice | solution.py:53
  452.7 0.8 copy-start.3
  453.9 2.9 copy-start.5
  462.1 1.6 copy-start.1
  463.6 1.0 copy-start.4
  463.6 1.2 copy-start.6
Sparse Core Ops, SparseCore 0:
  10.7 83.6 all-gather.1
  462.2 141.7 reduce-scatter.1
where the time goes:
time: 616 us; the launch traced here: 612 us
  local copies, waits for them, and re-layouts  369 us (60%)
  waiting for transfers between devices  139 us (23%)
  blocking collectives  73.6 us (12%)
  between operations  14.3 us (2%)
  other arithmetic  7.82 us (1%)
  matrix products  7.3 us (1%)
    gather x30, local copies, waits for them, and re-layouts, request_of(): return jnp.searchsorted(req_ends, positions, side='right')  363 us
    reduce_scatter x1, waiting for transfers between devices, body(): lax.psum_scatter(inv_temp * transposed(pos_coef, queries), 'batch', scatt...  138 us
    all_gather x1, blocking collectives, body(): bank_items = lax.all_gather(mem_items, 'mem', axis=0, tiled=True)  73.6 us
  transfers between devices with their start and end apart: 2, of which 1 were waited for; matrix products, arithmetic and copies ran while one was open for 61% of the time, Pallas kernels for 0%

commit v1 on v0

v1 whole, which is shorter than its diff:
```python
import jax
import jax.numpy as jnp
from jax import lax
from jax.experimental import pallas as pl
from jax.experimental.pallas import tpu as pltpu
from jax.sharding import PartitionSpec as P

MESH = pl.DeviceIdType.MESH
AGE_LIMIT = 16
NZ, NY, NH = 8, 8, 4
ROWS, DIM, HALF = 128, 256, 64
BLOCKS = 32
GROUP = ROWS * BLOCKS
SLOTS = 32
BANK = 1024
WINDOW = 34
TEMP = 8.0
UNIT = 1.0 / 1024.0
NEG = -1e30
FLOOR = -1e20
SEMS = 192
BF, F32 = jnp.bfloat16, jnp.float32


def nt(left, right):
    return lax.dot_general(left, right, (((1,), (1,)), ((), ())), preferred_element_type=F32)


def nn(left, right):
    return lax.dot_general(left, right, (((1,), (0,)), ((), ())), preferred_element_type=F32)


def iota(shape, dim):
    return lax.broadcasted_iota(jnp.int32, shape, dim)


def as_rows(row):
    return jnp.broadcast_to(row, (ROWS, ROWS)).T


def as_row(column):
    return jnp.broadcast_to(column, (ROWS, ROWS)).T[0:1, :]


def kernel(
    q_hbm, p_hbm, items_hbm, counts_hbm, ids_hbm, logq_hbm, bids_hbm, blogq_hbm, bage_hbm,
    loss_out, qgrad_out, pgrad_out,
    q_all, p_all, q_chip, p_chip, bank,
    s_ref, t_ref, e_ref, mx_ref,
    counts_v, ids_v, logq_v, bids_v, blogq_v, bage_v,
    hi_ref, lo_ref, dd_ref, idf, reqf, shf, wf, id_c, req_c, sh_c,
    stat_out, stat_in, lse_all, half_out, half_in, col_out, col_in, q_acc, p_acc,
    sm_ref, em_ref,
    send_sems, recv_sems, local_sems,
):
    b = lax.axis_index("batch")
    m = lax.axis_index("mem")
    core = lax.rem(b, 2)
    z = lax.rem(lax.div(b, 2), NZ)
    xl = lax.div(b, 2 * NZ)
    y = lax.rem(m, NY)
    xh = lax.div(m, NY)

    def on_batch(x_at, z_at, core_at):
        return {"batch": x_at * (2 * NZ) + z_at * 2 + core_at, "mem": m}

    def on_mem(h_at, y_at):
        return {"batch": b, "mem": h_at * NY + y_at}

    z_next = {1: lax.rem(z + 1, NZ), -1: lax.rem(z + NZ - 1, NZ)}
    y_next = {1: lax.rem(y + 1, NY), -1: lax.rem(y + NY - 1, NY)}
    z_dev = {s: on_batch(xl, z_next[s], core) for s in (1, -1)}
    y_dev = {s: on_mem(xh, y_next[s]) for s in (1, -1)}
    x_dev = on_batch(1 - xl, z, core)
    c_dev = on_batch(xl, z, 1 - core)
    h_dev = {e: on_mem(lax.rem(xh + e, NH), y) for e in (1, 2, 3)}

    copies = {}

    def send(key, src, dst, device):
        k = len(copies)
        copy = pltpu.make_async_remote_copy(
            src_ref=src,
            dst_ref=dst,
            send_sem=send_sems.at[k],
            recv_sem=recv_sems.at[k],
            device_id=device,
            device_id_type=MESH,
        )
        copy.start()
        copies[key] = copy

    local = []

    def load(src, dst):
        copy = pltpu.make_async_copy(src, dst, local_sems.at[len(local)])
        copy.start()
        local.append(copy)

    load(counts_hbm, counts_v)
    load(ids_hbm.at[pl.ds(m * BLOCKS, BLOCKS)], ids_v)
    load(logq_hbm.at[pl.ds(m * BLOCKS, BLOCKS)], logq_v)
    load(q_hbm, q_all.at[0])
    load(p_hbm, p_all.at[0])
    load(q_hbm, q_chip.at[0])
    load(p_hbm, p_chip.at[0])
    load(items_hbm, bank.at[m])
    load(bids_hbm.at[pl.ds(b * 8, 8)], bids_v)
    load(blogq_hbm.at[pl.ds(b * 8, 8)], blogq_v)
    load(bage_hbm.at[pl.ds(b * 8, 8)], bage_v)

    barrier = pltpu.get_barrier_semaphore()
    near = [z_dev[1], z_dev[-1], y_dev[1], y_dev[-1], x_dev, c_dev, h_dev[1], h_dev[2], h_dev[3]]
    for device in near:
        pl.semaphore_signal(barrier, inc=1, device_id=device, device_id_type=MESH)
    pl.semaphore_wait(barrier, len(near))

    own = {"q": q_hbm, "p": p_hbm}
    held = {"q": q_all, "p": p_all}
    last = {"p": {1: 4, -1: 3}, "q": {1: 3, -1: 4}}

    def piece(arr, col, h, d):
        rows = pl.ds(h * HALF, HALF)
        if col == 0 and d == 0:
            return own[arr].at[rows]
        return held[arr].at[2 * d + col, rows]

    def z_relay(arr, col, h, step, sign):
        if step >= last[arr][sign]:
            return
        here, there = (step * sign) % NZ, ((step + 1) * sign) % NZ
        dst = held[arr].at[2 * there + col, pl.ds(h * HALF, HALF)]
        send((arr, col, h, there), piece(arr, col, h, here), dst, z_dev[sign])

    def x_send(arr, h, d):
        dst = held[arr].at[2 * d + 1, pl.ds(h * HALF, HALF)]
        send((arr, "x", h, d), piece(arr, 0, h, d), dst, x_dev)

    def z_first(arr):
        for h in (0, 1):
            for sign in (1, -1):
                z_relay(arr, 0, h, 0, sign)

    def x_first(arr):
        x_send(arr, 0, 0)
        x_send(arr, 1, 0)

    def x_relay(arr):
        copies[arr, "x", 0, 0].wait_recv()
        for sign in (1, -1):
            z_relay(arr, 1, 0, 0, sign)

    def z_stage(arr, step):
        for col, h in ((0, 0), (0, 1), (1, 0)):
            for sign in (1, -1):
                if step > last[arr][sign]:
                    continue
                d = (step * sign) % NZ
                copies[arr, col, h, d].wait_recv()
                z_relay(arr, col, h, step, sign)
                if (col, h) == (0, 1):
                    x_send(arr, 1, d)

    def x_stage(arr, d):
        copies[arr, "x", 1, d].wait_recv()

    y_last = {0: {1: 4, -1: 3}, 1: {1: 4, -1: 3}, 2: {1: 3, -1: 4}, 3: {1: 3, -1: 4}}

    def bank_at(e, dy):
        return lax.rem(xh + NH - e, NH) * NY + lax.rem(y + NY - dy, NY)

    def y_relay(e, step, sign):
        if step >= y_last[e][sign]:
            return
        here, there = (step * sign) % NY, ((step + 1) * sign) % NY
        at = bank_at(e, here)
        src = items_hbm if (e, here) == (0, 0) else bank.at[at]
        send(("b", e, there), src, bank.at[at], y_dev[sign])

    def y_stage(e, step):
        for sign in (1, -1):
            if step > y_last[e][sign]:
                continue
            copies["b", e, (step * sign) % NY].wait_recv()
            y_relay(e, step, sign)

    def h_relay(e):
        copies["h", e].wait_recv()
        for sign in (1, -1):
            y_relay(e, 0, sign)

    z_first("p")
    x_first("p")
    for sign in (1, -1):
        y_relay(0, 0, sign)
    for e in (1, 3, 2):
        send(("h", e), items_hbm, bank.at[m], h_dev[e])
    send("cq", q_hbm, q_chip.at[1], c_dev)
    send("cp", p_hbm, p_chip.at[1], c_dev)
    z_first("q")
    x_first("q")

    for copy in local:
        copy.wait()
    sub, lane = iota((ROWS, ROWS), 0), iota((ROWS, ROWS), 1)
    upper = (sub <= lane).astype(F32).astype(BF)
    lower = (lane < sub).astype(F32).astype(BF)
    count = counts_v[...].astype(F32)
    count_bf = count.astype(BF)
    ends = nn(count_bf, upper) + jnp.sum(nn(lower, count_bf), axis=1, keepdims=True)
    ends = ends - (m * GROUP).astype(F32)
    starts = ends - count
    inside = (ends > 0.0) & (starts < float(GROUP))
    before = pltpu.roll(count, 1, 1)
    before = jnp.where(lane == 0, pltpu.roll(before, 1, 0), before)
    dd_ref[...] = jnp.where(starts <= 0.0, count, count - before)
    starts = jnp.maximum(starts, 0.0)
    high = jnp.floor(starts * (1.0 / ROWS))
    lo_ref[...] = starts - high * ROWS
    hi_ref[...] = jnp.where(inside, high, 999.0)
    passed = jnp.sum((ends[:, ROWS - 1 :] <= 0.0).astype(F32))
    first = jnp.minimum(passed.astype(jnp.int32), ROWS - WINDOW)
    sub32 = iota((BLOCKS, ROWS), 0).astype(F32)
    subf = sub.astype(F32)

    def scatter(step, total):
        lefts, rights = [], []
        for k in range(2):
            at = pl.ds(first + 2 * step + k, 1)
            same = hi_ref[at, :] == sub32
            mark = jnp.where(same, 1.0, 0.0)
            delta = jnp.where(same, dd_ref[at, :], 0.0)
            lefts.append(jnp.concatenate([mark, delta], axis=0).astype(BF))
            rights.append(jnp.where(lo_ref[at, :] == subf, 1.0, 0.0).astype(BF))
        return total + nt(jnp.concatenate(lefts, axis=1), jnp.concatenate(rights, axis=1))

    marks = lax.fori_loop(0, WINDOW // 2, scatter, jnp.zeros((2 * BLOCKS, ROWS), F32))
    low32 = (iota((BLOCKS, BLOCKS), 1) < iota((BLOCKS, BLOCKS), 0)).astype(F32).astype(BF)

    def running(part):
        part = part.astype(BF)
        return nn(part, upper) + jnp.sum(nn(low32, part), axis=1, keepdims=True)

    reqf[...] = running(marks[:BLOCKS])
    wf[...] = 1.0 / running(marks[BLOCKS:])
    idf[...] = ids_v[...].astype(F32)
    shf[...] = -logq_v[...].astype(F32) * UNIT
    chip_rows = (b, b + 1 - 2 * core)
    for k, at in enumerate(chip_rows):
        rows = pl.ds(k * ROWS, ROWS)
        id_c[rows, :] = as_rows(idf[pl.ds(at, 1), :])
        req_c[rows, :] = as_rows(reqf[pl.ds(at, 1), :])
        sh_c[rows, :] = as_rows(shf[pl.ds(at, 1), :])

    def pair_row(ref, d):
        z_at = lax.rem(z + NZ - d, NZ)
        parts = [ref[pl.ds(x_at * (2 * NZ) + z_at * 2 + core, 1), :] for x_at in (xl, 1 - xl)]
        return jnp.concatenate(parts, axis=1)

    def wide(ref):
        part = ref[...]
        return jnp.concatenate([part, part], axis=1)

    def keep_pair(d):
        keep = (wide(id_c) != pair_row(idf, d)) & (wide(req_c) != pair_row(reqf, d))
        if d == 0:
            keep = keep | (iota((2 * ROWS, 2 * ROWS), 0) == iota((2 * ROWS, 2 * ROWS), 1)) & (
                iota((2 * ROWS, 2 * ROWS), 0) < ROWS
            )
        return keep

    def both(ref):
        return ref[...].reshape(2 * ROWS, DIM)

    def pair(ref, d):
        return ref[2 * d : 2 * d + 2].reshape(2 * ROWS, DIM)

    def row_block(d):
        s = TEMP * nt(both(q_chip), pair(p_all, d)) + pair_row(shf, d)
        s = jnp.where(keep_pair(d), s, NEG)
        s_ref[d] = s
        top = jnp.maximum(s[:, :ROWS], s[:, ROWS:])
        mx_ref[...] = top if d == 0 else jnp.maximum(mx_ref[...], top)

    def col_block(d):
        t = TEMP * nt(both(p_chip), pair(q_all, d)) + wide(sh_c)
        t_ref[d] = jnp.where(keep_pair(d), t, NEG)

    x_relay("p")
    z_stage("p", 1)
    copies["cq"].wait_recv()
    copies["cp"].wait_recv()
    y_stage(0, 1)
    x_stage("p", 0)
    row_block(0)
    x_relay("q")
    z_stage("p", 2)
    h_relay(1)
    h_relay(3)
    x_stage("p", 1)
    row_block(1)
    x_stage("p", 7)
    row_block(7)
    y_stage(0, 2)
    z_stage("p", 3)
    h_relay(2)
    y_stage(1, 1)
    y_stage(3, 1)
    z_stage("q", 1)
    x_stage("p", 2)
    row_block(2)
    x_stage("p", 6)
    row_block(6)
    z_stage("p", 4)
    y_stage(0, 3)
    y_stage(2, 1)
    y_stage(1, 2)
    y_stage(3, 2)
    z_stage("q", 2)
    x_stage("p", 3)
    row_block(3)
    x_stage("p", 5)
    row_block(5)
    y_stage(0, 4)
    y_stage(2, 2)
    y_stage(1, 3)
    y_stage(3, 3)
    x_stage("p", 4)
    row_block(4)

    row_max = jnp.maximum(jnp.max(mx_ref[...], axis=1, keepdims=True), FLOOR)
    lane_sum = jnp.zeros((2 * ROWS, ROWS), F32)
    for d in range(NZ):
        e = jnp.exp(s_ref[d] - row_max)
        lane_sum = lane_sum + e[:, :ROWS] + e[:, ROWS:]
        e_ref[d] = e.astype(BF)
    row_sum = jnp.sum(lane_sum, axis=1, keepdims=True)
    max_a, sum_a = as_row(row_max[:ROWS]), as_row(row_sum[:ROWS])
    max_p, sum_p = as_row(row_max[ROWS:]), as_row(row_sum[ROWS:])
    stat_out[...] = jnp.where(iota((8, ROWS), 0) == 0, max_p, sum_p)
    send("stat", stat_out, stat_in, c_dev)

    z_stage("q", 3)
    y_stage(1, 4)
    y_stage(2, 3)
    y_stage(3, 4)
    y_stage(2, 4)

    q_own = q_chip[0]
    bank_max = None
    for k in range(BANK // ROWS):
        items = bank[4 * k : 4 * k + 4].reshape(ROWS, DIM)
        at = pl.ds(k, 1)
        shift = -blogq_v[at, :].astype(F32) * UNIT
        keep = (bids_v[at, :].astype(F32) != id_c[:ROWS, :]) & (bage_v[at, :] < AGE_LIMIT)
        s = jnp.where(keep, TEMP * nt(q_own, items) + shift, NEG)
        sm_ref[k] = s
        bank_max = s if k == 0 else jnp.maximum(bank_max, s)
    max_m = jnp.maximum(jnp.max(bank_max, axis=1, keepdims=True), FLOOR)
    lane_sum = jnp.zeros((ROWS, ROWS), F32)
    for k in range(BANK // ROWS):
        e = jnp.exp(sm_ref[k] - max_m)
        lane_sum = lane_sum + e
        em_ref[:, k * ROWS : (k + 1) * ROWS] = e.astype(BF)
    max_c, sum_c = as_row(max_m), as_row(jnp.sum(lane_sum, axis=1, keepdims=True))

    copies["stat"].wait_recv()
    max_b, sum_b = stat_in[0:1, :], stat_in[1:2, :]
    top = jnp.maximum(jnp.maximum(max_a, max_b), max_c)
    total = sum_a * jnp.exp(max_a - top) + sum_b * jnp.exp(max_b - top) + sum_c * jnp.exp(max_c - top)
    lse = top + jnp.log(total)
    lse_all[0] = jnp.broadcast_to(lse, (8, ROWS))
    for step in (4, 3, 2, 1, 0):
        for d in sorted({step, (NZ - step) % NZ}):
            for col in (1, 0):
                if (col, d) != (0, 0):
                    device = on_batch(xl if col == 0 else 1 - xl, lax.rem(z + d, NZ), core)
                    send(("lse", col, d), lse_all.at[0], lse_all.at[2 * d + col], device)

    z_stage("q", 4)
    for d in range(NZ):
        part = nn(e_ref[d], pair(p_all, d))
        q_acc[...] = part if d == 0 else q_acc[...] + part
    half_out[...] = q_acc[ROWS:, :]
    send("half", half_out, half_in, c_dev)
    mem_part = nn(em_ref[...], bank[...].reshape(BANK, DIM))

    x_stage("q", 0)
    col_block(0)
    for d in (1, 7, 2, 6, 3, 5, 4):
        x_stage("q", d)
        col_block(d)

    for d in (0, 1, 7, 2, 6, 3, 5, 4):
        for col in (0, 1):
            if (col, d) != (0, 0):
                copies["lse", col, d].wait_recv()
        level = jnp.concatenate([lse_all[2 * d][0:1, :], lse_all[2 * d + 1][0:1, :]], axis=1)
        coef = (jnp.exp(t_ref[d] - level) * pair_row(wf, d)).astype(BF)
        part = nn(coef, pair(q_all, d))
        p_acc[...] = part if d == 0 else p_acc[...] + part
    col_out[...] = p_acc[ROWS:, :]
    send("col", col_out, col_in, c_dev)

    weight = wf[pl.ds(b, 1), :]
    scale = TEMP * weight
    fact_a = as_rows(scale * jnp.exp(max_a - lse))[:, 0:1]
    fact_b = as_rows(scale * jnp.exp(max_b - lse))[:, 0:1]
    fact_c = as_rows(scale * jnp.exp(max_c - lse))[:, 0:1]
    own_term = as_rows(scale)[:, 0:1]
    q_f, p_f = q_chip[0].astype(F32), p_chip[0].astype(F32)
    copies["half"].wait_recv()
    qgrad_out[...] = (
        fact_a * q_acc[:ROWS, :] + fact_b * half_in[...] + fact_c * mem_part - own_term * p_f
    )
    own_logit = TEMP * as_row(jnp.sum(q_f * p_f, axis=1, keepdims=True)) + shf[pl.ds(b, 1), :]
    loss_out[...] = lse - own_logit
    copies["col"].wait_recv()
    pgrad_out[...] = TEMP * (p_acc[:ROWS, :] + col_in[...]) - own_term * q_f

    for copy in copies.values():
        copy.wait_send()


def body(queries, positives, pos_ids, pos_logq, mem_items, mem_ids, mem_logq, mem_age, counts):
    def lines(array):
        return array.reshape(-1, ROWS)

    any_spec = pl.BlockSpec(memory_space=pl.ANY)
    vmem_spec = pl.BlockSpec(memory_space=pltpu.VMEM)
    vmem = pltpu.VMEM
    scratch = [
        vmem((2 * NZ, ROWS, DIM), BF),
        vmem((2 * NZ, ROWS, DIM), BF),
        vmem((2, ROWS, DIM), BF),
        vmem((2, ROWS, DIM), BF),
        vmem((BLOCKS, SLOTS, DIM), BF),
        vmem((NZ, 2 * ROWS, 2 * ROWS), F32),
        vmem((NZ, 2 * ROWS, 2 * ROWS), F32),
        vmem((NZ, 2 * ROWS, 2 * ROWS), BF),
        vmem((2 * ROWS, ROWS), F32),
        vmem((ROWS, ROWS), jnp.int32),
        vmem((BLOCKS, ROWS), jnp.int32),
        vmem((BLOCKS, ROWS), jnp.int32),
        vmem((8, ROWS), jnp.int32),
        vmem((8, ROWS), jnp.int32),
        vmem((8, ROWS), jnp.int32),
        vmem((ROWS, ROWS), F32),
        vmem((ROWS, ROWS), F32),
        vmem((ROWS, ROWS), F32),
        vmem((BLOCKS, ROWS), F32),
        vmem((BLOCKS, ROWS), F32),
        vmem((BLOCKS, ROWS), F32),
        vmem((BLOCKS, ROWS), F32),
        vmem((2 * ROWS, ROWS), F32),
        vmem((2 * ROWS, ROWS), F32),
        vmem((2 * ROWS, ROWS), F32),
        vmem((8, ROWS), F32),
        vmem((8, ROWS), F32),
        vmem((2 * NZ, 8, ROWS), F32),
        vmem((ROWS, DIM), F32),
        vmem((ROWS, DIM), F32),
        vmem((ROWS, DIM), F32),
        vmem((ROWS, DIM), F32),
        vmem((2 * ROWS, DIM), F32),
        vmem((2 * ROWS, DIM), F32),
        vmem((BANK // ROWS, ROWS, ROWS), F32),
        vmem((ROWS, BANK), BF),
        pltpu.SemaphoreType.DMA((SEMS,)),
        pltpu.SemaphoreType.DMA((SEMS,)),
        pltpu.SemaphoreType.DMA((16,)),
    ]
    loss, query_grad, positive_grad = pl.pallas_call(
        kernel,
        out_shape=(
            jax.ShapeDtypeStruct((1, ROWS), F32),
            jax.ShapeDtypeStruct((ROWS, DIM), F32),
            jax.ShapeDtypeStruct((ROWS, DIM), F32),
        ),
        in_specs=[any_spec] * 9,
        out_specs=(vmem_spec, vmem_spec, vmem_spec),
        scratch_shapes=scratch,
        compiler_params=pltpu.CompilerParams(
            collective_id=0, has_side_effects=True, vmem_limit_bytes=40 << 20
        ),
        name="retrieval",
    )(
        queries, positives, mem_items, lines(counts), lines(pos_ids), lines(pos_logq),
        lines(mem_ids), lines(mem_logq), lines(mem_age),
    )
    return loss.reshape(ROWS), query_grad, positive_grad


def solution(mesh):
    in_specs = (
        P(("mem", "batch"), None),
        P(("mem", "batch"), None),
        P(),
        P(),
        P(("batch", "mem"), None),
        P(),
        P(),
        P(),
        P(),
    )
    out_specs = (P(("mem", "batch")), P(("mem", "batch"), None), P(("mem", "batch"), None))
    return jax.shard_map(body, mesh=mesh, in_specs=in_specs, out_specs=out_specs, check_vma=False)
```

time: 616 us -> 72.1 us (0.12)
  local copies, waits for them, and re-layouts: 369 us -> 9.84 us
  waiting for transfers between devices: 139 us -> 0 us
  blocking collectives: 73.6 us -> 0 us
  Pallas kernels: 0 us -> 61.1 us
  between operations: 14.3 us -> 0.66 us
  other arithmetic: 7.82 us -> 0 us
  matrix products: 7.3 us -> 0 us
    gather x31 -> x0, local copies, waits for them, and re-layouts: 364 us -> none  [the longest x30 363 us: request_of(): return jnp.searchsorted(req_ends, positions, side='right')]
    reduce_scatter x1 -> x0, waiting for transfers between devices: 138 us -> none  [body(): lax.psum_scatter(inv_temp * transposed(pos_coef, queries), 'batch', scatt...]
    all_gather x1 -> x0, blocking collectives: 73.6 us -> none  [body(): bank_items = lax.all_gather(mem_items, 'mem', axis=0, tiled=True)]
    pallas_call x0 -> x1, Pallas kernels: none -> 61.1 us  [body(): pl.pallas_call(kernel, out_shape=(jax.ShapeDtypeStruct((1, ROWS), F32), j...]
    dot_general x5 -> x0, matrix products: 7.3 us -> none  [the longest x2 3.22 us: scores(): lax.dot_general(left_mat, right_mat, (((1,), (1,)), ((), ())), preferred_...]
    unnamed x20 -> x21, local copies, waits for them, and re-layouts: 3.16 us -> 9.84 us
  transfers between devices with their start and end apart: 2 -> 0, of which waited for: 1 -> 0; matrix products, arithmetic and copies ran while one was open for 61% -> 0% of each run, Pallas kernels for 0% -> 0%
where the time goes in v1:
time: 72.1 us; the launch traced here: 71.6 us
  Pallas kernels  61.1 us (85%)
  local copies, waits for them, and re-layouts  9.84 us (14%)
    pallas_call x1, Pallas kernels, body(): pl.pallas_call(kernel, out_shape=(jax.ShapeDtypeStruct((1, ROWS), F32), j...  61.1 us
    unnamed x21, local copies, waits for them, and re-layouts  9.84 us

profile of v1, /device:TPU:1, one launch (start us, length us, event | category | flops | bytes accessed | tf_op | source)
XLA Modules:
  0.0 71.6 jit_solution(16188619175529935487)
XLA Ops:
  0.6 0.0 copy-start
  0.6 1.0 %copy-done = s32[131072]{0:T(1024)S(1)} copy-done((s32[131072]{0:T(1024)S(1)}, s32[131072]{0:T(1024)}, u32[]{:S(2)}) %copy-start) | copy-done | bytes 524312
  1.7 0.0 copy-start.1
  1.7 1.0 %copy-done.1 = s32[131072]{0:T(1024)S(1)} copy-done((s32[131072]{0:T(1024)S(1)}, s32[131072]{0:T(1024)}, u32[]{:S(2)}) %copy-start.1) | copy-done | bytes 524312
  2.7 0.0 copy-start.2
  2.7 0.9 %copy-done.2 = s32[32768]{0:T(1024)S(1)} copy-done((s32[32768]{0:T(1024)S(1)}, s32[32768]{0:T(1024)}, u32[]{:S(2)}) %copy-start.2) | copy-done | bytes 131096
  3.6 0.0 copy-start.3
  3.6 0.9 %copy-done.3 = s32[32768]{0:T(1024)S(1)} copy-done((s32[32768]{0:T(1024)S(1)}, s32[32768]{0:T(1024)}, u32[]{:S(2)}) %copy-start.3) | copy-done | bytes 131096
  4.5 0.0 copy-start.4
  4.5 0.9 %copy-done.4 = s32[32768]{0:T(1024)S(1)} copy-done((s32[32768]{0:T(1024)S(1)}, s32[32768]{0:T(1024)}, u32[]{:S(2)}) %copy-start.4) | copy-done | bytes 131096
  5.4 0.0 copy-start.5
  5.4 0.8 %copy-done.5 = bf16[128,256]{1,0:T(8,128)(2,1)S(1)} copy-done((bf16[128,256]{1,0:T(8,128)(2,1)S(1)}, bf16[128,256]{1,0:T(8,128)(2,1)}, u32[]{:S(2)}) %copy-start.5) | copy-done | bytes 65560
  6.3 0.0 copy-start.6
  6.3 0.8 %copy-done.6 = bf16[128,256]{1,0:T(8,128)(2,1)S(1)} copy-done((bf16[128,256]{1,0:T(8,128)(2,1)S(1)}, bf16[128,256]{1,0:T(8,128)(2,1)}, u32[]{:S(2)}) %copy-start.6) | copy-done | bytes 65560
  7.1 0.0 copy-start.7
  7.1 0.8 %copy-done.7 = s32[16384]{0:T(1024)S(1)} copy-done((s32[16384]{0:T(1024)S(1)}, s32[16384]{0:T(1024)}, u32[]{:S(2)}) %copy-start.7) | copy-done | bytes 65560
  8.0 0.0 copy-start.8
  8.0 0.7 copy-done.8
  8.7 61.1 %retrieval.1 = (f32[1,128]{1,0:T(1,128)S(1)}, f32[128,256]{1,0:T(8,128)S(1)}, f32[128,256]{1,0:T(8,128)S(1)}) custom-call(bf16[128,256]{1,0:T(8,128)(2,1)S(1)} %copy-done.5, bf16[128,256]{1,0:T(8,128)(2,1)S(1)} %copy-done.6, bf16[32,256]{1,0:T(8,128)(2,1)S(1)} %copy-done.8, s32[128,128]{1,0:T(8,128)S(1)} %bitcast.12, s32[1024,128]{1,0:T(8,128)S(1)} %bitcast.7, ...), custom_call_target="tpu_custom_call" | custom-call | tf_op jit(solution)/shard_map/retrieval/pallas_call | solution.py:473
  69.8 0.5 copy.15
  70.3 0.7 copy.16
  71.0 0.7 copy.17
Async XLA Ops:
  0.6 1.0 %copy-start = (s32[131072]{0:T(1024)S(1)}, s32[131072]{0:T(1024)}, u32[]{:S(2)}) copy-start(s32[131072]{0:T(1024)} %param.11) | copy-start | bytes 1572868
  1.7 1.0 %copy-start.1 = (s32[131072]{0:T(1024)S(1)}, s32[131072]{0:T(1024)}, u32[]{:S(2)}) copy-start(s32[131072]{0:T(1024)} %param.12) | copy-start | bytes 1572868
  2.7 0.9 %copy-start.2 = (s32[32768]{0:T(1024)S(1)}, s32[32768]{0:T(1024)}, u32[]{:S(2)}) copy-start(s32[32768]{0:T(1024)} %param.14) | copy-start | bytes 393220
  3.6 0.9 %copy-start.3 = (s32[32768]{0:T(1024)S(1)}, s32[32768]{0:T(1024)}, u32[]{:S(2)}) copy-start(s32[32768]{0:T(1024)} %param.15) | copy-start | bytes 393220
  4.5 0.9 %copy-start.4 = (s32[32768]{0:T(1024)S(1)}, s32[32768]{0:T(1024)}, u32[]{:S(2)}) copy-start(s32[32768]{0:T(1024)} %param.16) | copy-start | bytes 393220
  5.4 0.8 %copy-start.5 = (bf16[128,256]{1,0:T(8,128)(2,1)S(1)}, bf16[128,256]{1,0:T(8,128)(2,1)}, u32[]{:S(2)}) copy-start(bf16[128,256]{1,0:T(8,128)(2,1)} %q_hbm.1) | copy-start | bytes 196612
  6.3 0.8 %copy-start.6 = (bf16[128,256]{1,0:T(8,128)(2,1)S(1)}, bf16[128,256]{1,0:T(8,128)(2,1)}, u32[]{:S(2)}) copy-start(bf16[128,256]{1,0:T(8,128)(2,1)} %p_hbm.1) | copy-start | bytes 196612
  7.1 0.8 %copy-start.7 = (s32[16384]{0:T(1024)S(1)}, s32[16384]{0:T(1024)}, u32[]{:S(2)}) copy-start(s32[16384]{0:T(1024)} %param.17) | copy-start | bytes 196612
  8.0 0.7 %copy-start.8 = (bf16[32,256]{1,0:T(8,128)(2,1)S(1)}, bf16[32,256]{1,0:T(8,128)(2,1)}, u32[]{:S(2)}) copy-start(bf16[32,256]{1,0:T(8,128)(2,1)} %items_hbm.1) | copy-start | bytes 49156

commit v2 on v1

--- a/solution.py
+++ b/solution.py
@@ -18,7 +18,7 @@
 UNIT = 1.0 / 1024.0
 NEG = -1e30
 FLOOR = -1e20
-SEMS = 192
+SEMS = 136
 BF, F32 = jnp.bfloat16, jnp.float32
 
 
@@ -51,7 +51,7 @@
     hi_ref, lo_ref, dd_ref, idf, reqf, shf, wf, id_c, req_c, sh_c,
     stat_out, stat_in, lse_all, half_out, half_in, col_out, col_in, q_acc, p_acc,
     sm_ref, em_ref,
-    send_sems, recv_sems, local_sems,
+    send_sems, recv_sems, local_sems, token,
 ):
     b = lax.axis_index("batch")
     m = lax.axis_index("mem")
@@ -67,28 +67,33 @@
     def on_mem(h_at, y_at):
         return {"batch": b, "mem": h_at * NY + y_at}
 
-    z_next = {1: lax.rem(z + 1, NZ), -1: lax.rem(z + NZ - 1, NZ)}
-    y_next = {1: lax.rem(y + 1, NY), -1: lax.rem(y + NY - 1, NY)}
-    z_dev = {s: on_batch(xl, z_next[s], core) for s in (1, -1)}
-    y_dev = {s: on_mem(xh, y_next[s]) for s in (1, -1)}
     x_dev = on_batch(1 - xl, z, core)
     c_dev = on_batch(xl, z, 1 - core)
+    y_next = {1: lax.rem(y + 1, NY), -1: lax.rem(y + NY - 1, NY)}
+    y_dev = {s: on_mem(xh, y_next[s]) for s in (1, -1)}
     h_dev = {e: on_mem(lax.rem(xh + e, NH), y) for e in (1, 2, 3)}
-
-    copies = {}
-
-    def send(key, src, dst, device):
-        k = len(copies)
-        copy = pltpu.make_async_remote_copy(
+    z_up, z_down = lax.rem(z + 1, NZ), lax.rem(z + NZ - 1, NZ)
+    up_dev, down_dev = on_batch(xl, z_up, core), on_batch(xl, z_down, core)
+
+    sent = []
+
+    def remote(src, dst, send_at, recv_at, device):
+        return pltpu.make_async_remote_copy(
             src_ref=src,
             dst_ref=dst,
-            send_sem=send_sems.at[k],
-            recv_sem=recv_sems.at[k],
+            send_sem=send_sems.at[send_at],
+            recv_sem=recv_sems.at[recv_at],
             device_id=device,
             device_id_type=MESH,
         )
+
+    def send(src, dst, send_at, recv_at, device):
+        copy = remote(src, dst, send_at, recv_at, device)
         copy.start()
-        copies[key] = copy
+        sent.append((None, copy))
+
+    def received(ref, recv_at):
+        remote(ref, ref, 0, recv_at, x_dev).wait_recv()
 
     local = []
 
@@ -100,8 +105,8 @@
     load(counts_hbm, counts_v)
     load(ids_hbm.at[pl.ds(m * BLOCKS, BLOCKS)], ids_v)
     load(logq_hbm.at[pl.ds(m * BLOCKS, BLOCKS)], logq_v)
-    load(q_hbm, q_all.at[0])
-    load(p_hbm, p_all.at[0])
+    load(q_hbm, q_all.at[2 * z])
+    load(p_hbm, p_all.at[2 * z])
     load(q_hbm, q_chip.at[0])
     load(p_hbm, p_chip.at[0])
     load(items_hbm, bank.at[m])
@@ -110,59 +115,116 @@
     load(bage_hbm.at[pl.ds(b * 8, 8)], bage_v)
 
     barrier = pltpu.get_barrier_semaphore()
-    near = [z_dev[1], z_dev[-1], y_dev[1], y_dev[-1], x_dev, c_dev, h_dev[1], h_dev[2], h_dev[3]]
+
+    def greet(device):
+        pl.semaphore_signal(barrier, inc=1, device_id=device, device_id_type=MESH)
+
+    near = [x_dev, c_dev, y_dev[1], y_dev[-1], h_dev[1], h_dev[2], h_dev[3]]
     for device in near:
-        pl.semaphore_signal(barrier, inc=1, device_id=device, device_id_type=MESH)
-    pl.semaphore_wait(barrier, len(near))
+        greet(device)
+    pl.when(z < NZ - 1)(lambda: greet(up_dev))
+    pl.when(z > 0)(lambda: greet(down_dev))
+    pl.semaphore_wait(barrier, len(near) + (z < NZ - 1).astype(jnp.int32) + (z > 0).astype(jnp.int32))
+
+    @pl.when(z > 0)
+    def _():
+        pl.semaphore_wait(token, 1)
+
+    @pl.when(z < NZ - 1)
+    def _():
+        pl.semaphore_signal(token, inc=1, device_id=up_dev, device_id_type=MESH)
 
     own = {"q": q_hbm, "p": p_hbm}
     held = {"q": q_all, "p": p_all}
-    last = {"p": {1: 4, -1: 3}, "q": {1: 3, -1: 4}}
-
-    def piece(arr, col, h, d):
-        rows = pl.ds(h * HALF, HALF)
-        if col == 0 and d == 0:
-            return own[arr].at[rows]
-        return held[arr].at[2 * d + col, rows]
-
-    def z_relay(arr, col, h, step, sign):
-        if step >= last[arr][sign]:
-            return
-        here, there = (step * sign) % NZ, ((step + 1) * sign) % NZ
-        dst = held[arr].at[2 * there + col, pl.ds(h * HALF, HALF)]
-        send((arr, col, h, there), piece(arr, col, h, here), dst, z_dev[sign])
-
-    def x_send(arr, h, d):
-        dst = held[arr].at[2 * d + 1, pl.ds(h * HALF, HALF)]
-        send((arr, "x", h, d), piece(arr, 0, h, d), dst, x_dev)
-
-    def z_first(arr):
+    number = {"p": 0, "q": 1}
+    pieces = ((0, 0), (0, 1), (1, 0))
+    reach = (5, 5, 5, 4, 3, 2, 2, 2)
+
+    def half(arr, k, col, h):
+        return held[arr].at[2 * k + col, pl.ds(h * HALF, HALF)]
+
+    def z_recv(arr, k, piece):
+        return number[arr] * 24 + k * 3 + piece
+
+    own_z, own_x, relays, x_relays = {}, {}, {}, {}
+    for arr in ("p", "q"):
+        n = number[arr]
+        for piece, (col, h) in enumerate(pieces):
+            here = own[arr].at[pl.ds(h * HALF, HALF)] if col == 0 else half(arr, z, col, h)
+            for way, device in ((0, up_dev), (1, down_dev)):
+                own_z[arr, piece, way] = remote(
+                    here, half(arr, z, col, h), (n * 3 + piece) * 2 + way, z_recv(arr, z, piece), device
+                )
+            for k in range(NZ):
+                step = lax.rem(z - k + NZ, NZ)
+                target = jnp.where(step <= reach[k], z_up, z_down)
+                relays[arr, k, piece] = remote(
+                    half(arr, k, col, h), half(arr, k, col, h), 12 + n * 24 + k * 3 + piece,
+                    z_recv(arr, k, piece), on_batch(xl, target, core),
+                )
         for h in (0, 1):
-            for sign in (1, -1):
-                z_relay(arr, 0, h, 0, sign)
-
-    def x_first(arr):
-        x_send(arr, 0, 0)
-        x_send(arr, 1, 0)
-
-    def x_relay(arr):
-        copies[arr, "x", 0, 0].wait_recv()
-        for sign in (1, -1):
-            z_relay(arr, 1, 0, 0, sign)
-
-    def z_stage(arr, step):
-        for col, h in ((0, 0), (0, 1), (1, 0)):
-            for sign in (1, -1):
-                if step > last[arr][sign]:
-                    continue
-                d = (step * sign) % NZ
-                copies[arr, col, h, d].wait_recv()
-                z_relay(arr, col, h, step, sign)
-                if (col, h) == (0, 1):
-                    x_send(arr, 1, d)
-
-    def x_stage(arr, d):
-        copies[arr, "x", 1, d].wait_recv()
+            own_x[arr, h] = remote(
+                own[arr].at[pl.ds(h * HALF, HALF)], half(arr, z, 1, h),
+                76 + n if h == 0 else 60 + n * NZ + z, 64 + n if h == 0 else 48 + n * NZ + z, x_dev,
+            )
+        for k in range(NZ):
+            x_relays[arr, k] = remote(
+                half(arr, k, 0, 1), half(arr, k, 1, 1), 60 + n * NZ + k, 48 + n * NZ + k, x_dev
+            )
+
+    def begin(copy, when=None):
+        if when is None:
+            copy.start()
+        else:
+            pl.when(when)(copy.start)
+        sent.append((when, copy))
+
+    def own_first(arr):
+        for piece in (0, 1):
+            begin(own_z[arr, piece, 0])
+            begin(own_z[arr, piece, 1], z > 0)
+        for h in (0, 1):
+            begin(own_x[arr, h])
+
+    def own_second(arr):
+        received(half(arr, z, 1, 0), 64 + number[arr])
+        begin(own_z[arr, 2, 0])
+        begin(own_z[arr, 2, 1], z > 0)
+
+    def handle(arr, k, when, onward):
+        def steps():
+            for piece, (col, h) in enumerate(pieces):
+                received(half(arr, k, col, h), z_recv(arr, k, piece))
+                pl.when(onward)(relays[arr, k, piece].start)
+                if piece == 1:
+                    x_relays[arr, k].start()
+
+        pl.when(when)(steps)
+        for piece in range(3):
+            sent.append((when & onward, relays[arr, k, piece]))
+        sent.append((when, x_relays[arr, k]))
+
+    def line(arr, k, when=None):
+        step = lax.rem(z - k + NZ, NZ)
+        onward = ((step > 0) & (step < reach[k])) | (step > reach[k] + 1)
+        here = z != k
+        if k == 0:
+            here = here & (z < NZ - 2)
+        if k == 1:
+            here = here & (z < NZ - 1)
+            onward = onward & (z > 0)
+        handle(arr, k, here if when is None else here & when, onward)
+
+    def around(arr):
+        for piece in range(3):
+            begin(own_z[arr, piece, 1], z == 0)
+        for piece in range(3):
+            begin(relays[arr, 1, piece], z == 0)
+        handle(arr, 0, z >= NZ - 2, z == NZ - 1)
+        handle(arr, 1, z == NZ - 1, z < 0)
+
+    def x_stage(arr, k):
+        received(half(arr, k, 1, 1), 48 + number[arr] * NZ + k)
 
     y_last = {0: {1: 4, -1: 3}, 1: {1: 4, -1: 3}, 2: {1: 3, -1: 4}, 3: {1: 3, -1: 4}}
 
@@ -175,30 +237,29 @@
         here, there = (step * sign) % NY, ((step + 1) * sign) % NY
         at = bank_at(e, here)
         src = items_hbm if (e, here) == (0, 0) else bank.at[at]
-        send(("b", e, there), src, bank.at[at], y_dev[sign])
+        send(src, bank.at[at], 78 + e * NY + there, 66 + e * NY + there, y_dev[sign])
 
     def y_stage(e, step):
         for sign in (1, -1):
             if step > y_last[e][sign]:
                 continue
-            copies["b", e, (step * sign) % NY].wait_recv()
+            d = (step * sign) % NY
+            received(bank.at[bank_at(e, d)], 66 + e * NY + d)
             y_relay(e, step, sign)
 
     def h_relay(e):
-        copies["h", e].wait_recv()
+        received(bank.at[bank_at(e, 0)], 98 + e)
         for sign in (1, -1):
             y_relay(e, 0, sign)
 
-    z_first("p")
-    x_first("p")
+    own_first("p")
     for sign in (1, -1):
         y_relay(0, 0, sign)
     for e in (1, 3, 2):
-        send(("h", e), items_hbm, bank.at[m], h_dev[e])
-    send("cq", q_hbm, q_chip.at[1], c_dev)
-    send("cp", p_hbm, p_chip.at[1], c_dev)
-    z_first("q")
-    x_first("q")
+        send(items_hbm, bank.at[m], 110 + e, 98 + e, h_dev[e])
+    send(q_hbm, q_chip.at[1], 114, 102, c_dev)
+    send(p_hbm, p_chip.at[1], 115, 103, c_dev)
+    own_first("q")
 
     for copy in local:
         copy.wait()
@@ -252,22 +313,18 @@
         req_c[rows, :] = as_rows(reqf[pl.ds(at, 1), :])
         sh_c[rows, :] = as_rows(shf[pl.ds(at, 1), :])
 
-    def pair_row(ref, d):
-        z_at = lax.rem(z + NZ - d, NZ)
-        parts = [ref[pl.ds(x_at * (2 * NZ) + z_at * 2 + core, 1), :] for x_at in (xl, 1 - xl)]
+    def pair_row(ref, k):
+        parts = [ref[pl.ds(x_at * (2 * NZ) + k * 2 + core, 1), :] for x_at in (xl, 1 - xl)]
         return jnp.concatenate(parts, axis=1)
 
     def wide(ref):
         part = ref[...]
         return jnp.concatenate([part, part], axis=1)
 
-    def keep_pair(d):
-        keep = (wide(id_c) != pair_row(idf, d)) & (wide(req_c) != pair_row(reqf, d))
-        if d == 0:
-            keep = keep | (iota((2 * ROWS, 2 * ROWS), 0) == iota((2 * ROWS, 2 * ROWS), 1)) & (
-                iota((2 * ROWS, 2 * ROWS), 0) < ROWS
-            )
-        return keep
+    def keep_pair(k):
+        keep = (wide(id_c) != pair_row(idf, k)) & (wide(req_c) != pair_row(reqf, k))
+        left, right = iota((2 * ROWS, 2 * ROWS), 0), iota((2 * ROWS, 2 * ROWS), 1)
+        return keep | ((left == right + (z - k) * GROUP) & (left < ROWS))
 
     def both(ref):
         return ref[...].reshape(2 * ROWS, DIM)
@@ -275,58 +332,64 @@
     def pair(ref, d):
         return ref[2 * d : 2 * d + 2].reshape(2 * ROWS, DIM)
 
-    def row_block(d):
-        s = TEMP * nt(both(q_chip), pair(p_all, d)) + pair_row(shf, d)
-        s = jnp.where(keep_pair(d), s, NEG)
-        s_ref[d] = s
+    def row_block(k, first=False):
+        x_stage("p", k)
+        s = TEMP * nt(both(q_chip), pair(p_all, k)) + pair_row(shf, k)
+        s = jnp.where(keep_pair(k), s, NEG)
+        s_ref[k] = s
         top = jnp.maximum(s[:, :ROWS], s[:, ROWS:])
-        mx_ref[...] = top if d == 0 else jnp.maximum(mx_ref[...], top)
-
-    def col_block(d):
-        t = TEMP * nt(both(p_chip), pair(q_all, d)) + wide(sh_c)
-        t_ref[d] = jnp.where(keep_pair(d), t, NEG)
-
-    x_relay("p")
-    z_stage("p", 1)
-    copies["cq"].wait_recv()
-    copies["cp"].wait_recv()
+        mx_ref[...] = top if first else jnp.maximum(mx_ref[...], top)
+
+    def col_block(k):
+        x_stage("q", k)
+        t = TEMP * nt(both(p_chip), pair(q_all, k)) + wide(sh_c)
+        t_ref[k] = jnp.where(keep_pair(k), t, NEG)
+
+    early = z < 5
+    own_second("p")
+    line("p", 0)
+    line("p", 1)
     y_stage(0, 1)
-    x_stage("p", 0)
-    row_block(0)
-    x_relay("q")
-    z_stage("p", 2)
+    line("p", 2)
     h_relay(1)
     h_relay(3)
-    x_stage("p", 1)
-    row_block(1)
-    x_stage("p", 7)
-    row_block(7)
+    own_second("q")
+    line("p", 3)
     y_stage(0, 2)
-    z_stage("p", 3)
     h_relay(2)
+    received(q_chip.at[1], 102)
+    received(p_chip.at[1], 103)
+    row_block(2, True)
+    line("p", 4)
     y_stage(1, 1)
     y_stage(3, 1)
-    z_stage("q", 1)
-    x_stage("p", 2)
-    row_block(2)
-    x_stage("p", 6)
-    row_block(6)
-    z_stage("p", 4)
     y_stage(0, 3)
+    row_block(3)
+    line("p", 5)
     y_stage(2, 1)
     y_stage(1, 2)
     y_stage(3, 2)
-    z_stage("q", 2)
-    x_stage("p", 3)
-    row_block(3)
-    x_stage("p", 5)
+    y_stage(0, 4)
+    row_block(4)
+    for k in range(6):
+        line("q", k, early)
+    line("p", 6)
     row_block(5)
-    y_stage(0, 4)
+    line("q", 6)
     y_stage(2, 2)
     y_stage(1, 3)
     y_stage(3, 3)
-    x_stage("p", 4)
-    row_block(4)
+    line("p", 7)
+    row_block(6)
+    line("q", 7)
+    y_stage(2, 3)
+    y_stage(1, 4)
+    y_stage(3, 4)
+    row_block(7)
+    around("p")
+    y_stage(2, 4)
+    row_block(0)
+    row_block(1)
 
     row_max = jnp.maximum(jnp.max(mx_ref[...], axis=1, keepdims=True), FLOOR)
     lane_sum = jnp.zeros((2 * ROWS, ROWS), F32)
@@ -338,13 +401,7 @@
     max_a, sum_a = as_row(row_max[:ROWS]), as_row(row_sum[:ROWS])
     max_p, sum_p = as_row(row_max[ROWS:]), as_row(row_sum[ROWS:])
     stat_out[...] = jnp.where(iota((8, ROWS), 0) == 0, max_p, sum_p)
-    send("stat", stat_out, stat_in, c_dev)
-
-    z_stage("q", 3)
-    y_stage(1, 4)
-    y_stage(2, 3)
-    y_stage(3, 4)
-    y_stage(2, 4)
+    send(stat_out, stat_in, 116, 104, c_dev)
 
     q_own = q_chip[0]
     bank_max = None
@@ -364,43 +421,41 @@
         em_ref[:, k * ROWS : (k + 1) * ROWS] = e.astype(BF)
     max_c, sum_c = as_row(max_m), as_row(jnp.sum(lane_sum, axis=1, keepdims=True))
 
-    copies["stat"].wait_recv()
+    received(stat_in, 104)
     max_b, sum_b = stat_in[0:1, :], stat_in[1:2, :]
     top = jnp.maximum(jnp.maximum(max_a, max_b), max_c)
     total = sum_a * jnp.exp(max_a - top) + sum_b * jnp.exp(max_b - top) + sum_c * jnp.exp(max_c - top)
     lse = top + jnp.log(total)
-    lse_all[0] = jnp.broadcast_to(lse, (8, ROWS))
-    for step in (4, 3, 2, 1, 0):
-        for d in sorted({step, (NZ - step) % NZ}):
-            for col in (1, 0):
-                if (col, d) != (0, 0):
-                    device = on_batch(xl if col == 0 else 1 - xl, lax.rem(z + d, NZ), core)
-                    send(("lse", col, d), lse_all.at[0], lse_all.at[2 * d + col], device)
-
-    z_stage("q", 4)
+    lse_all[2 * z] = jnp.broadcast_to(lse, (8, ROWS))
+    for step in (1, 7, 2, 6, 3, 5, 4, 0):
+        for col in (0, 1):
+            if (col, step) != (0, 0):
+                device = on_batch(xl if col == 0 else 1 - xl, lax.rem(z + step, NZ), core)
+                at = 2 * z + col
+                send(lse_all.at[2 * z], lse_all.at[at], 119 + 2 * step + col, 107 + at, device)
+
+    for k in range(6):
+        line("q", k, z >= 5)
+    around("q")
     for d in range(NZ):
         part = nn(e_ref[d], pair(p_all, d))
         q_acc[...] = part if d == 0 else q_acc[...] + part
     half_out[...] = q_acc[ROWS:, :]
-    send("half", half_out, half_in, c_dev)
+    send(half_out, half_in, 117, 105, c_dev)
     mem_part = nn(em_ref[...], bank[...].reshape(BANK, DIM))
 
-    x_stage("q", 0)
-    col_block(0)
-    for d in (1, 7, 2, 6, 3, 5, 4):
-        x_stage("q", d)
-        col_block(d)
-
-    for d in (0, 1, 7, 2, 6, 3, 5, 4):
-        for col in (0, 1):
-            if (col, d) != (0, 0):
-                copies["lse", col, d].wait_recv()
-        level = jnp.concatenate([lse_all[2 * d][0:1, :], lse_all[2 * d + 1][0:1, :]], axis=1)
-        coef = (jnp.exp(t_ref[d] - level) * pair_row(wf, d)).astype(BF)
-        part = nn(coef, pair(q_all, d))
-        p_acc[...] = part if d == 0 else p_acc[...] + part
+    for k in range(NZ):
+        col_block(k)
+
+    for k in range(NZ):
+        pl.when(z != k)(lambda k=k: received(lse_all.at[2 * k], 107 + 2 * k))
+        received(lse_all.at[2 * k + 1], 108 + 2 * k)
+        level = jnp.concatenate([lse_all[2 * k][0:1, :], lse_all[2 * k + 1][0:1, :]], axis=1)
+        coef = (jnp.exp(t_ref[k] - level) * pair_row(wf, k)).astype(BF)
+        part = nn(coef, pair(q_all, k))
+        p_acc[...] = part if k == 0 else p_acc[...] + part
     col_out[...] = p_acc[ROWS:, :]
-    send("col", col_out, col_in, c_dev)
+    send(col_out, col_in, 118, 106, c_dev)
 
     weight = wf[pl.ds(b, 1), :]
     scale = TEMP * weight
@@ -409,24 +464,27 @@
     fact_c = as_rows(scale * jnp.exp(max_c - lse))[:, 0:1]
     own_term = as_rows(scale)[:, 0:1]
     q_f, p_f = q_chip[0].astype(F32), p_chip[0].astype(F32)
-    copies["half"].wait_recv()
+    received(half_in, 105)
     qgrad_out[...] = (
         fact_a * q_acc[:ROWS, :] + fact_b * half_in[...] + fact_c * mem_part - own_term * p_f
     )
     own_logit = TEMP * as_row(jnp.sum(q_f * p_f, axis=1, keepdims=True)) + shf[pl.ds(b, 1), :]
     loss_out[...] = lse - own_logit
-    copies["col"].wait_recv()
+    received(col_in, 106)
     pgrad_out[...] = TEMP * (p_acc[:ROWS, :] + col_in[...]) - own_term * q_f
 
-    for copy in copies.values():
-        copy.wait_send()
+    for when, copy in sent:
+        if when is None:
+            copy.wait_send()
+        else:
+            pl.when(when)(copy.wait_send)
 
 
 def body(queries, positives, pos_ids, pos_logq, mem_items, mem_ids, mem_logq, mem_age, counts):
     def lines(array):
         return array.reshape(-1, ROWS)
 
-    any_spec = pl.BlockSpec(memory_space=pl.ANY)
+    any_spec = pl.BlockSpec(memory_space=pltpu.HBM)
     vmem_spec = pl.BlockSpec(memory_space=pltpu.VMEM)
     vmem = pltpu.VMEM
     scratch = [
@@ -469,6 +527,7 @@
         pltpu.SemaphoreType.DMA((SEMS,)),
         pltpu.SemaphoreType.DMA((SEMS,)),
         pltpu.SemaphoreType.DMA((16,)),
+        pltpu.SemaphoreType.REGULAR,
     ]
     loss, query_grad, positive_grad = pl.pallas_call(
         kernel,
@@ -481,7 +540,7 @@
         out_specs=(vmem_spec, vmem_spec, vmem_spec),
         scratch_shapes=scratch,
         compiler_params=pltpu.CompilerParams(
-            collective_id=0, has_side_effects=True, vmem_limit_bytes=40 << 20
+            collective_id=0, has_side_effects=True, vmem_limit_bytes=67043328
         ),
         name="retrieval",
     )(

time: 72.1 us -> 109 us (1.51)
  the two profiles are of different devices: /device:TPU:1 before, /device:TPU:769 now
where the time goes in v2:
time: 109 us; the launch traced here: 108 us
  Pallas kernels  104 us (95%)
  local copies, waits for them, and re-layouts  3.44 us (3%)
    pallas_call x1, Pallas kernels, body(): pl.pallas_call(kernel, out_shape=(jax.ShapeDtypeStruct((1, ROWS), F32), j...  104 us
    unnamed x7, local copies, waits for them, and re-layouts  3.44 us

profile of v2, /device:TPU:769, one launch (start us, length us, event | category | flops | bytes accessed | tf_op | source)
XLA Modules:
  0.0 108.5 jit_solution(4045942387727233438)
XLA Ops:
  0.6 104.4 %retrieval.1 = (f32[1,128]{1,0:T(1,128)}, f32[128,256]{1,0:T(8,128)}, f32[128,256]{1,0:T(8,128)}) custom-call(bf16[128,256]{1,0:T(8,128)(2,1)} %q_hbm.1, bf16[128,256]{1,0:T(8,128)(2,1)} %p_hbm.1, bf16[32,256]{1,0:T(8,128)(2,1)} %items_hbm.1, s32[128,128]{1,0:T(8,128)} %bitcast.12, s32[1024,128]{1,0:T(8,128)} %bitcast.7, s32[1024,128]{1,0:T(8,128)} %bitcast.8, ...), custom_call_target="tpu_custom_call" | custom-call | tf_op jit(solution)/shard_map/retrieval/pallas_call | solution.py:532
  105.0 0.0 copy-start.1
  105.0 0.7 copy-done.1
  105.7 0.5 copy.15
  106.2 0.0 copy-start
  106.2 1.6 %copy.16 = f32[128,256]{1,0:T(8,128)} copy(f32[128,256]{1,0:T(8,128)} %get-tuple-element.13) | data formatting | bytes 262144
  107.8 0.0 copy-done
  107.8 0.7 copy.17
Async XLA Ops:
  105.0 0.7 copy-start.1
  106.2 1.6 %copy-start = (f32[128,256]{1,0:T(8,128)S(1)}, f32[128,256]{1,0:T(8,128)}, u32[]{:S(2)}) copy-start(f32[128,256]{1,0:T(8,128)} %get-tuple-element.14) | copy-start | bytes 393220

commit v3 on v1

--- a/solution.py
+++ b/solution.py
@@ -8,7 +8,7 @@
 MESH = pl.DeviceIdType.MESH
 AGE_LIMIT = 16
 NZ, NY, NH = 8, 8, 4
-ROWS, DIM, HALF = 128, 256, 64
+ROWS, DIM, CUT = 128, 256, 32
 BLOCKS = 32
 GROUP = ROWS * BLOCKS
 SLOTS = 32
@@ -67,10 +67,12 @@
     def on_mem(h_at, y_at):
         return {"batch": b, "mem": h_at * NY + y_at}
 
-    z_next = {1: lax.rem(z + 1, NZ), -1: lax.rem(z + NZ - 1, NZ)}
-    y_next = {1: lax.rem(y + 1, NY), -1: lax.rem(y + NY - 1, NY)}
-    z_dev = {s: on_batch(xl, z_next[s], core) for s in (1, -1)}
-    y_dev = {s: on_mem(xh, y_next[s]) for s in (1, -1)}
+    def z_dev(hop):
+        return on_batch(xl, lax.rem(z + hop + NZ, NZ), core)
+
+    def y_dev(hop):
+        return on_mem(xh, lax.rem(y + hop + NY, NY))
+
     x_dev = on_batch(1 - xl, z, core)
     c_dev = on_batch(xl, z, 1 - core)
     h_dev = {e: on_mem(lax.rem(xh + e, NH), y) for e in (1, 2, 3)}
@@ -110,95 +112,94 @@
     load(bage_hbm.at[pl.ds(b * 8, 8)], bage_v)
 
     barrier = pltpu.get_barrier_semaphore()
-    near = [z_dev[1], z_dev[-1], y_dev[1], y_dev[-1], x_dev, c_dev, h_dev[1], h_dev[2], h_dev[3]]
+    near = [place(hop) for place in (z_dev, y_dev) for hop in (1, -1, 2, -2)]
+    near += [x_dev, c_dev, h_dev[1], h_dev[2], h_dev[3]]
     for device in near:
         pl.semaphore_signal(barrier, inc=1, device_id=device, device_id_type=MESH)
     pl.semaphore_wait(barrier, len(near))
 
     own = {"q": q_hbm, "p": p_hbm}
     held = {"q": q_all, "p": p_all}
-    last = {"p": {1: 4, -1: 3}, "q": {1: 3, -1: 4}}
-
-    def piece(arr, col, h, d):
-        rows = pl.ds(h * HALF, HALF)
+    onward = {"p": ((2, 1), (2, 2), (6, -1)), "q": ((2, 1), (6, -1), (6, -2))}
+
+    def got(*key):
+        copies[key].wait_recv()
+
+    def piece(arr, col, d):
         if col == 0 and d == 0:
-            return own[arr].at[rows]
-        return held[arr].at[2 * d + col, rows]
-
-    def z_relay(arr, col, h, step, sign):
-        if step >= last[arr][sign]:
-            return
-        here, there = (step * sign) % NZ, ((step + 1) * sign) % NZ
-        dst = held[arr].at[2 * there + col, pl.ds(h * HALF, HALF)]
-        send((arr, col, h, there), piece(arr, col, h, here), dst, z_dev[sign])
-
-    def x_send(arr, h, d):
-        dst = held[arr].at[2 * d + 1, pl.ds(h * HALF, HALF)]
-        send((arr, "x", h, d), piece(arr, 0, h, d), dst, x_dev)
-
-    def z_first(arr):
-        for h in (0, 1):
-            for sign in (1, -1):
-                z_relay(arr, 0, h, 0, sign)
+            return own[arr]
+        return held[arr].at[2 * d] if col == 0 else held[arr].at[2 * d + 1, pl.ds(0, CUT)]
+
+    def z_send(arr, col, d, hop):
+        there = (d + hop) % NZ
+        block = held[arr].at[2 * there + col]
+        dst = block if col == 0 else held[arr].at[2 * there + 1, pl.ds(0, CUT)]
+        send((arr, col, there), piece(arr, col, d), dst, z_dev(hop))
+
+    def z_first(arr, col, hops):
+        for hop in hops:
+            z_send(arr, col, 0, hop)
+
+    def z_relay(arr, col):
+        for d in (2, 6):
+            got(arr, col, d)
+            for start, hop in onward[arr]:
+                if start == d:
+                    z_send(arr, col, d, hop)
 
     def x_first(arr):
-        x_send(arr, 0, 0)
-        x_send(arr, 1, 0)
-
-    def x_relay(arr):
-        copies[arr, "x", 0, 0].wait_recv()
-        for sign in (1, -1):
-            z_relay(arr, 1, 0, 0, sign)
-
-    def z_stage(arr, step):
-        for col, h in ((0, 0), (0, 1), (1, 0)):
-            for sign in (1, -1):
-                if step > last[arr][sign]:
-                    continue
-                d = (step * sign) % NZ
-                copies[arr, col, h, d].wait_recv()
-                z_relay(arr, col, h, step, sign)
-                if (col, h) == (0, 1):
-                    x_send(arr, 1, d)
-
-    def x_stage(arr, d):
-        copies[arr, "x", 1, d].wait_recv()
-
-    y_last = {0: {1: 4, -1: 3}, 1: {1: 4, -1: 3}, 2: {1: 3, -1: 4}, 3: {1: 3, -1: 4}}
+        src, dst = own[arr].at[pl.ds(0, CUT)], held[arr].at[1, pl.ds(0, CUT)]
+        send((arr, "first"), src, dst, x_dev)
+
+    def x_send(arr, d):
+        rest = pl.ds(CUT, ROWS - CUT)
+        src = own[arr].at[rest] if d == 0 else held[arr].at[2 * d, rest]
+        send((arr, "x", d), src, held[arr].at[2 * d + 1, rest], x_dev)
+
+    def x_pass(arr, *blocks):
+        for d in blocks:
+            if d not in (2, 6):
+                got(arr, 0, d)
+            x_send(arr, d)
+
+    def second(arr):
+        got(arr, "first")
+        z_first(arr, 1, (1, -1, 2, -2))
+
+    def have(arr, d):
+        got(arr, "x", d)
+        if d not in (0, 2, 6):
+            got(arr, 1, d)
 
     def bank_at(e, dy):
         return lax.rem(xh + NH - e, NH) * NY + lax.rem(y + NY - dy, NY)
 
-    def y_relay(e, step, sign):
-        if step >= y_last[e][sign]:
-            return
-        here, there = (step * sign) % NY, ((step + 1) * sign) % NY
-        at = bank_at(e, here)
-        src = items_hbm if (e, here) == (0, 0) else bank.at[at]
-        send(("b", e, there), src, bank.at[at], y_dev[sign])
-
-    def y_stage(e, step):
-        for sign in (1, -1):
-            if step > y_last[e][sign]:
-                continue
-            copies["b", e, (step * sign) % NY].wait_recv()
-            y_relay(e, step, sign)
-
-    def h_relay(e):
-        copies["h", e].wait_recv()
-        for sign in (1, -1):
-            y_relay(e, 0, sign)
-
-    z_first("p")
+    def y_send(e, d, hop):
+        at = bank_at(e, d)
+        src = items_hbm if (e, d) == (0, 0) else bank.at[at]
+        send(("b", e, (d + hop) % NY), src, bank.at[at], y_dev(hop))
+
+    def y_first(e):
+        if e:
+            got("h", e)
+        for hop in (1, -1, 2, -2):
+            y_send(e, 0, hop)
+
+    def y_relay(e):
+        for d, hop in ((2, 1), (2, 2), (6, -1)) if e in (0, 1) else ((2, 1), (6, -1), (6, -2)):
+            if (d, hop) != (2, 2) and (d, hop) != (6, -2):
+                got("b", e, d)
+            y_send(e, d, hop)
+
+    z_first("p", 0, (2, -2, 1, -1))
     x_first("p")
-    for sign in (1, -1):
-        y_relay(0, 0, sign)
     for e in (1, 3, 2):
         send(("h", e), items_hbm, bank.at[m], h_dev[e])
-    send("cq", q_hbm, q_chip.at[1], c_dev)
-    send("cp", p_hbm, p_chip.at[1], c_dev)
-    z_first("q")
-    x_first("q")
+    y_first(0)
+    x_send("p", 0)
+    send(("cq",), q_hbm, q_chip.at[1], c_dev)
+    send(("cp",), p_hbm, p_chip.at[1], c_dev)
+    z_first("q", 0, (1, -1))
 
     for copy in local:
         copy.wait()
@@ -276,6 +277,7 @@
         return ref[2 * d : 2 * d + 2].reshape(2 * ROWS, DIM)
 
     def row_block(d):
+        have("p", d)
         s = TEMP * nt(both(q_chip), pair(p_all, d)) + pair_row(shf, d)
         s = jnp.where(keep_pair(d), s, NEG)
         s_ref[d] = s
@@ -283,49 +285,41 @@
         mx_ref[...] = top if d == 0 else jnp.maximum(mx_ref[...], top)
 
     def col_block(d):
+        have("q", d)
         t = TEMP * nt(both(p_chip), pair(q_all, d)) + wide(sh_c)
         t_ref[d] = jnp.where(keep_pair(d), t, NEG)
 
-    x_relay("p")
-    z_stage("p", 1)
-    copies["cq"].wait_recv()
-    copies["cp"].wait_recv()
-    y_stage(0, 1)
-    x_stage("p", 0)
+    second("p")
+    x_pass("p", 1, 7)
+    y_first(1)
+    y_first(3)
+    z_relay("p", 0)
+    y_relay(0)
+    x_pass("p", 2, 6)
+    y_first(2)
+    z_relay("p", 1)
+    z_first("q", 0, (2, -2))
+    x_first("q")
+    x_send("q", 0)
+    got("cq")
+    got("cp")
     row_block(0)
-    x_relay("q")
-    z_stage("p", 2)
-    h_relay(1)
-    h_relay(3)
-    x_stage("p", 1)
     row_block(1)
-    x_stage("p", 7)
     row_block(7)
-    y_stage(0, 2)
-    z_stage("p", 3)
-    h_relay(2)
-    y_stage(1, 1)
-    y_stage(3, 1)
-    z_stage("q", 1)
-    x_stage("p", 2)
+    y_relay(1)
+    y_relay(3)
+    x_pass("p", 3, 5)
+    second("q")
+    x_pass("p", 4)
     row_block(2)
-    x_stage("p", 6)
     row_block(6)
-    z_stage("p", 4)
-    y_stage(0, 3)
-    y_stage(2, 1)
-    y_stage(1, 2)
-    y_stage(3, 2)
-    z_stage("q", 2)
-    x_stage("p", 3)
+    y_relay(2)
+    x_pass("q", 1, 7)
+    z_relay("q", 0)
+    x_pass("q", 2, 6)
     row_block(3)
-    x_stage("p", 5)
     row_block(5)
-    y_stage(0, 4)
-    y_stage(2, 2)
-    y_stage(1, 3)
-    y_stage(3, 3)
-    x_stage("p", 4)
+    z_relay("q", 1)
     row_block(4)
 
     row_max = jnp.maximum(jnp.max(mx_ref[...], axis=1, keepdims=True), FLOOR)
@@ -338,13 +332,12 @@
     max_a, sum_a = as_row(row_max[:ROWS]), as_row(row_sum[:ROWS])
     max_p, sum_p = as_row(row_max[ROWS:]), as_row(row_sum[ROWS:])
     stat_out[...] = jnp.where(iota((8, ROWS), 0) == 0, max_p, sum_p)
-    send("stat", stat_out, stat_in, c_dev)
-
-    z_stage("q", 3)
-    y_stage(1, 4)
-    y_stage(2, 3)
-    y_stage(3, 4)
-    y_stage(2, 4)
+    send(("stat",), stat_out, stat_in, c_dev)
+
+    x_pass("q", 3, 5, 4)
+    for e in range(NH):
+        for d in (1, 7, 3, 5, 4):
+            got("b", e, d)
 
     q_own = q_chip[0]
     bank_max = None
@@ -364,43 +357,38 @@
         em_ref[:, k * ROWS : (k + 1) * ROWS] = e.astype(BF)
     max_c, sum_c = as_row(max_m), as_row(jnp.sum(lane_sum, axis=1, keepdims=True))
 
-    copies["stat"].wait_recv()
+    got("stat")
     max_b, sum_b = stat_in[0:1, :], stat_in[1:2, :]
     top = jnp.maximum(jnp.maximum(max_a, max_b), max_c)
     total = sum_a * jnp.exp(max_a - top) + sum_b * jnp.exp(max_b - top) + sum_c * jnp.exp(max_c - top)
     lse = top + jnp.log(total)
     lse_all[0] = jnp.broadcast_to(lse, (8, ROWS))
-    for step in (4, 3, 2, 1, 0):
-        for d in sorted({step, (NZ - step) % NZ}):
-            for col in (1, 0):
-                if (col, d) != (0, 0):
-                    device = on_batch(xl if col == 0 else 1 - xl, lax.rem(z + d, NZ), core)
-                    send(("lse", col, d), lse_all.at[0], lse_all.at[2 * d + col], device)
-
-    z_stage("q", 4)
+    for d in (4, 3, 5, 2, 6, 1, 7, 0):
+        for col in (1, 0):
+            if (col, d) != (0, 0):
+                device = on_batch(xl if col == 0 else 1 - xl, lax.rem(z + d, NZ), core)
+                send(("lse", col, d), lse_all.at[0], lse_all.at[2 * d + col], device)
+
     for d in range(NZ):
         part = nn(e_ref[d], pair(p_all, d))
         q_acc[...] = part if d == 0 else q_acc[...] + part
     half_out[...] = q_acc[ROWS:, :]
-    send("half", half_out, half_in, c_dev)
+    send(("half",), half_out, half_in, c_dev)
     mem_part = nn(em_ref[...], bank[...].reshape(BANK, DIM))
 
-    x_stage("q", 0)
-    col_block(0)
-    for d in (1, 7, 2, 6, 3, 5, 4):
-        x_stage("q", d)
+    for d in (0, 1, 7, 2, 6, 3, 5, 4):
         col_block(d)
 
     for d in (0, 1, 7, 2, 6, 3, 5, 4):
         for col in (0, 1):
             if (col, d) != (0, 0):
-                copies["lse", col, d].wait_recv()
+                got("lse", col, d)
         level = jnp.concatenate([lse_all[2 * d][0:1, :], lse_all[2 * d + 1][0:1, :]], axis=1)
         coef = (jnp.exp(t_ref[d] - level) * pair_row(wf, d)).astype(BF)
         part = nn(coef, pair(q_all, d))
         p_acc[...] = part if d == 0 else p_acc[...] + part
     col_out[...] = p_acc[ROWS:, :]
-    send("col", col_out, col_in, c_dev)
+    send(("col",), col_out, col_in, c_dev)
 
     weight = wf[pl.ds(b, 1), :]
     scale = TEMP * weight
@@ -409,13 +397,13 @@
     fact_c = as_rows(scale * jnp.exp(max_c - lse))[:, 0:1]
     own_term = as_rows(scale)[:, 0:1]
     q_f, p_f = q_chip[0].astype(F32), p_chip[0].astype(F32)
-    copies["half"].wait_recv()
+    got("half")
     qgrad_out[...] = (
         fact_a * q_acc[:ROWS, :] + fact_b * half_in[...] + fact_c * mem_part - own_term * p_f
     )
     own_logit = TEMP * as_row(jnp.sum(q_f * p_f, axis=1, keepdims=True)) + shf[pl.ds(b, 1), :]
     loss_out[...] = lse - own_logit
-    copies["col"].wait_recv()
+    got("col")
     pgrad_out[...] = TEMP * (p_acc[:ROWS, :] + col_in[...]) - own_term * q_f
 
     for copy in copies.values():
@@ -426,7 +414,7 @@
     def lines(array):
         return array.reshape(-1, ROWS)
 
-    any_spec = pl.BlockSpec(memory_space=pl.ANY)
+    any_spec = pl.BlockSpec(memory_space=pltpu.HBM)
     vmem_spec = pl.BlockSpec(memory_space=pltpu.VMEM)
     vmem = pltpu.VMEM
     scratch = [
@@ -481,7 +469,7 @@
         out_specs=(vmem_spec, vmem_spec, vmem_spec),
         scratch_shapes=scratch,
         compiler_params=pltpu.CompilerParams(
-            collective_id=0, has_side_effects=True, vmem_limit_bytes=40 << 20
+            collective_id=0, has_side_effects=True, vmem_limit_bytes=67043328
         ),
         name="retrieval",
     )(

time: 72.1 us -> 59.8 us (0.83)
  local copies, waits for them, and re-layouts: 9.84 us -> 3.44 us
  Pallas kernels: 61.1 us -> 55.6 us
    unnamed x21 -> x7, local copies, waits for them, and re-layouts: 9.84 us -> 3.44 us
    pallas_call x1, Pallas kernels: 61.1 us -> 55.6 us  [body(): pl.pallas_call(kernel, out_shape=(jax.ShapeDtypeStruct((1, ROWS), F32), j...]
where the time goes in v3:
time: 59.8 us; the launch traced here: 59.6 us
  Pallas kernels  55.6 us (93%)
  local copies, waits for them, and re-layouts  3.44 us (6%)
  between operations  0.65 us (1%)
    pallas_call x1, Pallas kernels, body(): pl.pallas_call(kernel, out_shape=(jax.ShapeDtypeStruct((1, ROWS), F32), j...  55.6 us
    unnamed x7, local copies, waits for them, and re-layouts  3.44 us

profile of v3, /device:TPU:1, one launch (start us, length us, event | category | flops | bytes accessed | tf_op | source)
XLA Modules:
  0.0 59.6 jit_solution(10733648769199144614)
XLA Ops:
  0.6 55.6 %retrieval.1 = (f32[1,128]{1,0:T(1,128)}, f32[128,256]{1,0:T(8,128)}, f32[128,256]{1,0:T(8,128)}) custom-call(bf16[128,256]{1,0:T(8,128)(2,1)} %q_hbm.1, bf16[128,256]{1,0:T(8,128)(2,1)} %p_hbm.1, bf16[32,256]{1,0:T(8,128)(2,1)} %items_hbm.1, s32[128,128]{1,0:T(8,128)} %bitcast.12, s32[1024,128]{1,0:T(8,128)} %bitcast.7, s32[1024,128]{1,0:T(8,128)} %bitcast.8, ...), custom_call_target="tpu_custom_call" | custom-call | tf_op jit(solution)/shard_map/retrieval/pallas_call | solution.py:461
  56.2 0.0 copy-start.1
  56.2 0.7 %copy-done.1 = f32[1,128]{1,0:T(1,128)S(1)} copy-done((f32[1,128]{1,0:T(1,128)S(1)}, f32[1,128]{1,0:T(1,128)}, u32[]{:S(2)}) %copy-start.1) | copy-done | bytes 536
  56.9 0.5 copy.15
  57.4 0.0 copy-start
  57.4 1.6 %copy.16 = f32[128,256]{1,0:T(8,128)} copy(f32[128,256]{1,0:T(8,128)} %get-tuple-element.13) | data formatting | bytes 262144
  59.0 0.0 copy-done
  59.0 0.7 %copy.17 = f32[128,256]{1,0:T(8,128)} copy(f32[128,256]{1,0:T(8,128)S(1)} %copy-done) | data formatting | bytes 262144
Async XLA Ops:
  56.2 0.7 %copy-start.1 = (f32[1,128]{1,0:T(1,128)S(1)}, f32[1,128]{1,0:T(1,128)}, u32[]{:S(2)}) copy-start(f32[1,128]{1,0:T(1,128)} %get-tuple-element.6) | copy-start | bytes 1540
  57.4 1.6 %copy-start = (f32[128,256]{1,0:T(8,128)S(1)}, f32[128,256]{1,0:T(8,128)}, u32[]{:S(2)}) copy-start(f32[128,256]{1,0:T(8,128)} %get-tuple-element.14) | copy-start | bytes 393220

commit v4 on v3

--- a/solution.py
+++ b/solution.py
@@ -18,7 +18,7 @@
 UNIT = 1.0 / 1024.0
 NEG = -1e30
 FLOOR = -1e20
-SEMS = 192
+SENDS, ARRIVALS, LOADS = 8, 40, 5
 BF, F32 = jnp.bfloat16, jnp.float32
 
 
@@ -47,7 +47,7 @@
     loss_out, qgrad_out, pgrad_out,
     q_all, p_all, q_chip, p_chip, bank,
     s_ref, t_ref, e_ref, mx_ref,
-    counts_v, ids_v, logq_v, bids_v, blogq_v, bage_v,
+    counts_v, lines_v, bank_v,
     hi_ref, lo_ref, dd_ref, idf, reqf, shf, wf, id_c, req_c, sh_c,
     stat_out, stat_in, lse_all, half_out, half_in, col_out, col_in, q_acc, p_acc,
     sm_ref, em_ref,
@@ -75,45 +75,47 @@
 
     x_dev = on_batch(1 - xl, z, core)
     c_dev = on_batch(xl, z, 1 - core)
-    h_dev = {e: on_mem(lax.rem(xh + e, NH), y) for e in (1, 2, 3)}
-
-    copies = {}
-
-    def send(key, src, dst, device):
-        k = len(copies)
-        copy = pltpu.make_async_remote_copy(
+    h_dev = {e: on_mem(lax.rem(xh + e, NH), y) for e in (1, 3)}
+
+    send_at, arrive_at = {}, {}
+
+    def send(out, into, src, dst, device):
+        pltpu.make_async_remote_copy(
             src_ref=src,
             dst_ref=dst,
-            send_sem=send_sems.at[k],
-            recv_sem=recv_sems.at[k],
+            send_sem=send_sems.at[send_at.setdefault(out, len(send_at))],
+            recv_sem=recv_sems.at[arrive_at.setdefault(into, len(arrive_at))],
             device_id=device,
             device_id_type=MESH,
-        )
-        copy.start()
-        copies[key] = copy
-
-    local = []
-
-    def load(src, dst):
-        copy = pltpu.make_async_copy(src, dst, local_sems.at[len(local)])
-        copy.start()
-        local.append(copy)
-
-    load(counts_hbm, counts_v)
-    load(ids_hbm.at[pl.ds(m * BLOCKS, BLOCKS)], ids_v)
-    load(logq_hbm.at[pl.ds(m * BLOCKS, BLOCKS)], logq_v)
-    load(q_hbm, q_all.at[0])
-    load(p_hbm, p_all.at[0])
-    load(q_hbm, q_chip.at[0])
-    load(p_hbm, p_chip.at[0])
-    load(items_hbm, bank.at[m])
-    load(bids_hbm.at[pl.ds(b * 8, 8)], bids_v)
-    load(blogq_hbm.at[pl.ds(b * 8, 8)], blogq_v)
-    load(bage_hbm.at[pl.ds(b * 8, 8)], bage_v)
+        ).start()
+
+    def waiting(sem, ref):
+        pltpu.make_async_copy(ref, ref, sem).wait()
+
+    def sent(out, ref):
+        waiting(send_sems.at[send_at[out]], ref)
+
+    def got(into, ref):
+        waiting(recv_sems.at[arrive_at[into]], ref)
+
+    def load(kind, src, dst):
+        pltpu.make_async_copy(src, dst, local_sems.at[kind]).start()
+
+    load(0, counts_hbm, counts_v)
+    load(1, ids_hbm.at[pl.ds(m * BLOCKS, BLOCKS)], lines_v.at[0])
+    load(1, logq_hbm.at[pl.ds(m * BLOCKS, BLOCKS)], lines_v.at[1])
+    load(2, bids_hbm.at[pl.ds(b * 8, 8)], bank_v.at[0])
+    load(2, blogq_hbm.at[pl.ds(b * 8, 8)], bank_v.at[1])
+    load(2, bage_hbm.at[pl.ds(b * 8, 8)], bank_v.at[2])
+    load(3, q_hbm, q_all.at[0])
+    load(3, p_hbm, p_all.at[0])
+    load(3, q_hbm, q_chip.at[0])
+    load(3, p_hbm, p_chip.at[0])
+    load(4, items_hbm, bank.at[m])
 
     barrier = pltpu.get_barrier_semaphore()
     near = [place(hop) for place in (z_dev, y_dev) for hop in (1, -1, 2, -2)]
-    near += [x_dev, c_dev, h_dev[1], h_dev[2], h_dev[3]]
+    near += [x_dev, c_dev, h_dev[1], h_dev[3]]
     for device in near:
         pl.semaphore_signal(barrier, inc=1, device_id=device, device_id_type=MESH)
     pl.semaphore_wait(barrier, len(near))
@@ -122,87 +124,103 @@
     held = {"q": q_all, "p": p_all}
     onward = {"p": ((2, 1), (2, 2), (6, -1)), "q": ((2, 1), (6, -1), (6, -2))}
 
-    def got(*key):
-        copies[key].wait_recv()
+    def blocks(arr, n):
+        return held[arr].at[pl.ds(0, n)]
 
     def piece(arr, col, d):
         if col == 0 and d == 0:
             return own[arr]
         return held[arr].at[2 * d] if col == 0 else held[arr].at[2 * d + 1, pl.ds(0, CUT)]
 
+    near_far = {1: 1, 7: 1, 2: 2, 6: 2, 3: 3, 5: 3, 4: 3}
+    final = {1: "near", 7: "near", 3: "far", 5: "far", 4: "last"}
+
     def z_send(arr, col, d, hop):
         there = (d + hop) % NZ
         block = held[arr].at[2 * there + col]
         dst = block if col == 0 else held[arr].at[2 * there + 1, pl.ds(0, CUT)]
-        send((arr, col, there), piece(arr, col, d), dst, z_dev(hop))
+        into = near_far[there] if col == 0 else final.get(there, "cut")
+        send(arr, (arr, into), piece(arr, col, d), dst, z_dev(hop))
 
     def z_first(arr, col, hops):
         for hop in hops:
             z_send(arr, col, 0, hop)
 
     def z_relay(arr, col):
-        for d in (2, 6):
-            got(arr, col, d)
-            for start, hop in onward[arr]:
-                if start == d:
-                    z_send(arr, col, d, hop)
+        got((arr, 2), blocks(arr, 2)) if col == 0 else got((arr, "cut"), held[arr].at[1, pl.ds(0, 2 * CUT)])
+        for d, hop in onward[arr]:
+            z_send(arr, col, d, hop)
 
     def x_first(arr):
         src, dst = own[arr].at[pl.ds(0, CUT)], held[arr].at[1, pl.ds(0, CUT)]
-        send((arr, "first"), src, dst, x_dev)
+        send(arr, (arr, "first"), src, dst, x_dev)
 
     def x_send(arr, d):
         rest = pl.ds(CUT, ROWS - CUT)
         src = own[arr].at[rest] if d == 0 else held[arr].at[2 * d, rest]
-        send((arr, "x", d), src, held[arr].at[2 * d + 1, rest], x_dev)
-
-    def x_pass(arr, *blocks):
-        for d in blocks:
-            if d not in (2, 6):
-                got(arr, 0, d)
+        into = final.get(d, "x0" if d == 0 else "x2")
+        send(arr, (arr, into), src, held[arr].at[2 * d + 1, rest], x_dev)
+
+    def x_pass(arr, *group):
+        if group[0] == 1:
+            got((arr, 1), blocks(arr, 2))
+        if group[0] == 3:
+            got((arr, 3), blocks(arr, 3))
+        for d in group:
             x_send(arr, d)
 
     def second(arr):
-        got(arr, "first")
+        got((arr, "first"), held[arr].at[1, pl.ds(0, CUT)])
         z_first(arr, 1, (1, -1, 2, -2))
 
     def have(arr, d):
-        got(arr, "x", d)
-        if d not in (0, 2, 6):
-            got(arr, 1, d)
+        rest = ROWS - CUT
+        if d == 0:
+            got((arr, "x0"), held[arr].at[1, pl.ds(0, rest)])
+        if d == 2:
+            got((arr, "x2"), held[arr].at[pl.ds(0, 2), pl.ds(0, rest)])
+        if d in (1, 3):
+            got((arr, final[d]), blocks(arr, 2))
+        if d == 4:
+            got((arr, final[d]), blocks(arr, 1))
 
     def bank_at(e, dy):
         return lax.rem(xh + NH - e, NH) * NY + lax.rem(y + NY - dy, NY)
 
     def y_send(e, d, hop):
-        at = bank_at(e, d)
+        at, there = bank_at(e, d), (d + hop) % NY
         src = items_hbm if (e, d) == (0, 0) else bank.at[at]
-        send(("b", e, (d + hop) % NY), src, bank.at[at], y_dev(hop))
+        into = ("bank", e) if there in (2, 6) else "bank"
+        send("bank", into, src, bank.at[at], y_dev(hop))
 
     def y_first(e):
         if e:
-            got("h", e)
+            got(("h", e), bank.at[0])
+        if e == 1:
+            send("bank", ("h", 2), bank.at[bank_at(1, 0)], bank.at[bank_at(1, 0)], h_dev[1])
         for hop in (1, -1, 2, -2):
             y_send(e, 0, hop)
 
     def y_relay(e):
+        got(("bank", e), bank.at[pl.ds(0, 2)])
         for d, hop in ((2, 1), (2, 2), (6, -1)) if e in (0, 1) else ((2, 1), (6, -1), (6, -2)):
-            if (d, hop) != (2, 2) and (d, hop) != (6, -2):
-                got("b", e, d)
             y_send(e, d, hop)
 
     z_first("p", 0, (2, -2, 1, -1))
     x_first("p")
-    for e in (1, 3, 2):
-        send(("h", e), items_hbm, bank.at[m], h_dev[e])
+    for e in (1, 3):
+        send("bank", ("h", e), items_hbm, bank.at[m], h_dev[e])
     y_first(0)
     x_send("p", 0)
-    send(("cq",), q_hbm, q_chip.at[1], c_dev)
-    send(("cp",), p_hbm, p_chip.at[1], c_dev)
+    send("chip", "chip", q_hbm, q_chip.at[1], c_dev)
+    send("chip", "chip", p_hbm, p_chip.at[1], c_dev)
     z_first("q", 0, (1, -1))
 
-    for copy in local:
-        copy.wait()
+    waiting(local_sems.at[0], counts_v)
+    waiting(local_sems.at[1], lines_v)
+    waiting(local_sems.at[2], bank_v)
+    waiting(local_sems.at[3], blocks("q", 4))
+    waiting(local_sems.at[4], bank.at[0])
     sub, lane = iota((ROWS, ROWS), 0), iota((ROWS, ROWS), 1)
     upper = (sub <= lane).astype(F32).astype(BF)
     lower = (lane < sub).astype(F32).astype(BF)
@@ -244,8 +262,8 @@
 
     reqf[...] = running(marks[:BLOCKS])
     wf[...] = 1.0 / running(marks[BLOCKS:])
-    idf[...] = ids_v[...].astype(F32)
-    shf[...] = -logq_v[...].astype(F32) * UNIT
+    idf[...] = lines_v[0].astype(F32)
+    shf[...] = -lines_v[1].astype(F32) * UNIT
     chip_rows = (b, b + 1 - 2 * core)
     for k, at in enumerate(chip_rows):
         rows = pl.ds(k * ROWS, ROWS)
@@ -301,8 +319,7 @@
     z_first("q", 0, (2, -2))
     x_first("q")
     x_send("q", 0)
-    got("cq")
-    got("cp")
+    got("chip", q_chip)
     row_block(0)
     row_block(1)
     row_block(7)
@@ -332,20 +349,18 @@
     max_a, sum_a = as_row(row_max[:ROWS]), as_row(row_sum[:ROWS])
     max_p, sum_p = as_row(row_max[ROWS:]), as_row(row_sum[ROWS:])
     stat_out[...] = jnp.where(iota((8, ROWS), 0) == 0, max_p, sum_p)
-    send(("stat",), stat_out, stat_in, c_dev)
+    send("stat", "stat", stat_out, stat_in, c_dev)
 
     x_pass("q", 3, 5, 4)
-    for e in range(NH):
-        for d in (1, 7, 3, 5, 4):
-            got("b", e, d)
+    got("bank", bank.at[pl.ds(0, 5 * NH)])
 
     q_own = q_chip[0]
     bank_max = None
     for k in range(BANK // ROWS):
         items = bank[4 * k : 4 * k + 4].reshape(ROWS, DIM)
         at = pl.ds(k, 1)
-        shift = -blogq_v[at, :].astype(F32) * UNIT
-        keep = (bids_v[at, :].astype(F32) != id_c[:ROWS, :]) & (bage_v[at, :] < AGE_LIMIT)
+        shift = -bank_v[1, at, :].astype(F32) * UNIT
+        keep = (bank_v[0, at, :].astype(F32) != id_c[:ROWS, :]) & (bank_v[2, at, :] < AGE_LIMIT)
         s = jnp.where(keep, TEMP * nt(q_own, items) + shift, NEG)
         sm_ref[k] = s
         bank_max = s if k == 0 else jnp.maximum(bank_max, s)
@@ -357,7 +372,7 @@
         em_ref[:, k * ROWS : (k + 1) * ROWS] = e.astype(BF)
     max_c, sum_c = as_row(max_m), as_row(jnp.sum(lane_sum, axis=1, keepdims=True))
 
-    got("stat")
+    got("stat", stat_in)
     max_b, sum_b = stat_in[0:1, :], stat_in[1:2, :]
     top = jnp.maximum(jnp.maximum(max_a, max_b), max_c)
     total = sum_a * jnp.exp(max_a - top) + sum_b * jnp.exp(max_b - top) + sum_c * jnp.exp(max_c - top)
@@ -367,28 +382,29 @@
         for col in (1, 0):
             if (col, d) != (0, 0):
                 device = on_batch(xl if col == 0 else 1 - xl, lax.rem(z + d, NZ), core)
-                send(("lse", col, d), lse_all.at[0], lse_all.at[2 * d + col], device)
+                send("lse", ("lse", d in (3, 4, 5)), lse_all.at[0], lse_all.at[2 * d + col], device)
 
     for d in range(NZ):
         part = nn(e_ref[d], pair(p_all, d))
         q_acc[...] = part if d == 0 else q_acc[...] + part
     half_out[...] = q_acc[ROWS:, :]
-    send(("half",), half_out, half_in, c_dev)
+    send("half", "half", half_out, half_in, c_dev)
     mem_part = nn(em_ref[...], bank[...].reshape(BANK, DIM))
 
     for d in (0, 1, 7, 2, 6, 3, 5, 4):
         col_block(d)
 
     for d in (0, 1, 7, 2, 6, 3, 5, 4):
-        for col in (0, 1):
-            if (col, d) != (0, 0):
-                got("lse", col, d)
+        if d == 0:
+            got(("lse", False), lse_all.at[pl.ds(0, 9)])
+        if d == 3:
+            got(("lse", True), lse_all.at[pl.ds(0, 6)])
         level = jnp.concatenate([lse_all[2 * d][0:1, :], lse_all[2 * d + 1][0:1, :]], axis=1)
         coef = (jnp.exp(t_ref[d] - level) * pair_row(wf, d)).astype(BF)
         part = nn(coef, pair(q_all, d))
         p_acc[...] = part if d == 0 else p_acc[...] + part
     col_out[...] = p_acc[ROWS:, :]
-    send(("col",), col_out, col_in, c_dev)
+    send("col", "col", col_out, col_in, c_dev)
 
     weight = wf[pl.ds(b, 1), :]
     scale = TEMP * weight
@@ -397,17 +413,21 @@
     fact_c = as_rows(scale * jnp.exp(max_c - lse))[:, 0:1]
     own_term = as_rows(scale)[:, 0:1]
     q_f, p_f = q_chip[0].astype(F32), p_chip[0].astype(F32)
-    got("half")
+    got("half", half_in)
     qgrad_out[...] = (
         fact_a * q_acc[:ROWS, :] + fact_b * half_in[...] + fact_c * mem_part - own_term * p_f
     )
     own_logit = TEMP * as_row(jnp.sum(q_f * p_f, axis=1, keepdims=True)) + shf[pl.ds(b, 1), :]
     loss_out[...] = lse - own_logit
-    got("col")
+    got("col", col_in)
     pgrad_out[...] = TEMP * (p_acc[:ROWS, :] + col_in[...]) - own_term * q_f
 
-    for copy in copies.values():
-        copy.wait_send()
+    for out, ref in (
+        ("p", blocks("p", 15)), ("q", blocks("q", 15)), ("bank", bank.at[pl.ds(0, 31)]),
+        ("lse", lse_all.at[pl.ds(0, 15)]), ("chip", q_chip), ("stat", stat_out), ("half", half_out),
+        ("col", col_out),
+    ):
+        sent(out, ref)
 
 
 def body(queries, positives, pos_ids, pos_logq, mem_items, mem_ids, mem_logq, mem_age, counts):
@@ -428,11 +448,8 @@
         vmem((NZ, 2 * ROWS, 2 * ROWS), BF),
         vmem((2 * ROWS, ROWS), F32),
         vmem((ROWS, ROWS), jnp.int32),
-        vmem((BLOCKS, ROWS), jnp.int32),
-        vmem((BLOCKS, ROWS), jnp.int32),
-        vmem((8, ROWS), jnp.int32),
-        vmem((8, ROWS), jnp.int32),
-        vmem((8, ROWS), jnp.int32),
+        vmem((2, BLOCKS, ROWS), jnp.int32),
+        vmem((3, 8, ROWS), jnp.int32),
         vmem((ROWS, ROWS), F32),
         vmem((ROWS, ROWS), F32),
         vmem((ROWS, ROWS), F32),
@@ -454,9 +471,9 @@
         vmem((2 * ROWS, DIM), F32),
         vmem((BANK // ROWS, ROWS, ROWS), F32),
         vmem((ROWS, BANK), BF),
-        pltpu.SemaphoreType.DMA((SEMS,)),
-        pltpu.SemaphoreType.DMA((SEMS,)),
-        pltpu.SemaphoreType.DMA((16,)),
+        pltpu.SemaphoreType.DMA((SENDS,)),
+        pltpu.SemaphoreType.DMA((ARRIVALS,)),
+        pltpu.SemaphoreType.DMA((LOADS,)),
     ]
     loss, query_grad, positive_grad = pl.pallas_call(
         kernel,

time: 59.8 us -> 58.2 us (0.973)
  Pallas kernels: 55.6 us -> 53.6 us
    pallas_call x1, Pallas kernels: 55.6 us -> 53.6 us  [body(): pl.pallas_call(kernel, out_shape=(jax.ShapeDtypeStruct((1, ROWS), F32), j...]
where the time goes in v4:
time: 58.2 us; the launch traced here: 57.7 us
  Pallas kernels  53.6 us (92%)
  local copies, waits for them, and re-layouts  3.44 us (6%)
  between operations  0.65 us (1%)
    pallas_call x1, Pallas kernels, body(): pl.pallas_call(kernel, out_shape=(jax.ShapeDtypeStruct((1, ROWS), F32), j...  53.6 us
    unnamed x7, local copies, waits for them, and re-layouts  3.44 us

profile of v4, /device:TPU:1, one launch (start us, length us, event | category | flops | bytes accessed | tf_op | source)
XLA Modules:
  0.0 57.7 jit_solution(3089367169276774863)
XLA Ops:
  0.6 53.6 %retrieval.1 = (f32[1,128]{1,0:T(1,128)}, f32[128,256]{1,0:T(8,128)}, f32[128,256]{1,0:T(8,128)}) custom-call(bf16[128,256]{1,0:T(8,128)(2,1)} %q_hbm.1, bf16[128,256]{1,0:T(8,128)(2,1)} %p_hbm.1, bf16[32,256]{1,0:T(8,128)(2,1)} %items_hbm.1, s32[128,128]{1,0:T(8,128)} %bitcast.12, s32[1024,128]{1,0:T(8,128)} %bitcast.7, s32[1024,128]{1,0:T(8,128)} %bitcast.8, ...), custom_call_target="tpu_custom_call" | custom-call | tf_op jit(solution)/shard_map/retrieval/pallas_call | solution.py:478
  54.2 0.0 copy-start.1
  54.2 0.7 %copy-done.1 = f32[1,128]{1,0:T(1,128)S(1)} copy-done((f32[1,128]{1,0:T(1,128)S(1)}, f32[1,128]{1,0:T(1,128)}, u32[]{:S(2)}) %copy-start.1) | copy-done | bytes 536
  54.9 0.5 copy.15
  55.4 0.0 copy-start
  55.4 1.6 %copy.16 = f32[128,256]{1,0:T(8,128)} copy(f32[128,256]{1,0:T(8,128)} %get-tuple-element.13) | data formatting | bytes 262144
  57.0 0.0 copy-done
  57.0 0.7 %copy.17 = f32[128,256]{1,0:T(8,128)} copy(f32[128,256]{1,0:T(8,128)S(1)} %copy-done) | data formatting | bytes 262144
Async XLA Ops:
  54.2 0.7 %copy-start.1 = (f32[1,128]{1,0:T(1,128)S(1)}, f32[1,128]{1,0:T(1,128)}, u32[]{:S(2)}) copy-start(f32[1,128]{1,0:T(1,128)} %get-tuple-element.6) | copy-start | bytes 1540
  55.4 1.6 %copy-start = (f32[128,256]{1,0:T(8,128)S(1)}, f32[128,256]{1,0:T(8,128)}, u32[]{:S(2)}) copy-start(f32[128,256]{1,0:T(8,128)} %get-tuple-element.14) | copy-start | bytes 393220

commit v5 on v4

--- a/solution.py
+++ b/solution.py
@@ -18,7 +18,7 @@
 UNIT = 1.0 / 1024.0
 NEG = -1e30
 FLOOR = -1e20
-SENDS, ARRIVALS, LOADS = 8, 40, 5
+SENDS, ARRIVALS, LOADS = 8, 42, 5
 BF, F32 = jnp.bfloat16, jnp.float32
 
 
@@ -113,11 +113,65 @@
     load(3, p_hbm, p_chip.at[0])
     load(4, items_hbm, bank.at[m])
 
+    def requests():
+        waiting(local_sems.at[0], counts_v)
+        waiting(local_sems.at[1], lines_v)
+        sub, lane = iota((ROWS, ROWS), 0), iota((ROWS, ROWS), 1)
+        upper = (sub <= lane).astype(F32).astype(BF)
+        lower = (lane < sub).astype(F32).astype(BF)
+        count = counts_v[...].astype(F32)
+        count_bf = count.astype(BF)
+        ends = nn(count_bf, upper) + jnp.sum(nn(lower, count_bf), axis=1, keepdims=True)
+        ends = ends - (m * GROUP).astype(F32)
+        starts = ends - count
+        inside = (ends > 0.0) & (starts < float(GROUP))
+        before = pltpu.roll(count, 1, 1)
+        before = jnp.where(lane == 0, pltpu.roll(before, 1, 0), before)
+        dd_ref[...] = jnp.where(starts <= 0.0, count, count - before)
+        starts = jnp.maximum(starts, 0.0)
+        high = jnp.floor(starts * (1.0 / ROWS))
+        lo_ref[...] = starts - high * ROWS
+        hi_ref[...] = jnp.where(inside, high, 999.0)
+        passed = jnp.sum((ends[:, ROWS - 1 :] <= 0.0).astype(F32))
+        first = jnp.minimum(passed.astype(jnp.int32), ROWS - WINDOW)
+        sub32 = iota((BLOCKS, ROWS), 0).astype(F32)
+        subf = sub.astype(F32)
+
+        def scatter(step, total):
+            lefts, rights = [], []
+            for k in range(2):
+                at = pl.ds(first + 2 * step + k, 1)
+                same = hi_ref[at, :] == sub32
+                mark = jnp.where(same, 1.0, 0.0)
+                delta = jnp.where(same, dd_ref[at, :], 0.0)
+                lefts.append(jnp.concatenate([mark, delta], axis=0).astype(BF))
+                rights.append(jnp.where(lo_ref[at, :] == subf, 1.0, 0.0).astype(BF))
+            return total + nt(jnp.concatenate(lefts, axis=1), jnp.concatenate(rights, axis=1))
+
+        marks = lax.fori_loop(0, WINDOW // 2, scatter, jnp.zeros((2 * BLOCKS, ROWS), F32))
+        low32 = (iota((BLOCKS, BLOCKS), 1) < iota((BLOCKS, BLOCKS), 0)).astype(F32).astype(BF)
+
+        def running(part):
+            part = part.astype(BF)
+            return nn(part, upper) + jnp.sum(nn(low32, part), axis=1, keepdims=True)
+
+        reqf[...] = running(marks[:BLOCKS])
+        wf[...] = 1.0 / running(marks[BLOCKS:])
+        idf[...] = lines_v[0].astype(F32)
+        shf[...] = -lines_v[1].astype(F32) * UNIT
+        chip_rows = (b, b + 1 - 2 * core)
+        for k, at in enumerate(chip_rows):
+            rows = pl.ds(k * ROWS, ROWS)
+            id_c[rows, :] = as_rows(idf[pl.ds(at, 1), :])
+            req_c[rows, :] = as_rows(reqf[pl.ds(at, 1), :])
+            sh_c[rows, :] = as_rows(shf[pl.ds(at, 1), :])
+
     barrier = pltpu.get_barrier_semaphore()
     near = [place(hop) for place in (z_dev, y_dev) for hop in (1, -1, 2, -2)]
     near += [x_dev, c_dev, h_dev[1], h_dev[3]]
     for device in near:
         pl.semaphore_signal(barrier, inc=1, device_id=device, device_id_type=MESH)
+    pl.when(z < 6)(requests)
     pl.semaphore_wait(barrier, len(near))
 
     own = {"q": q_hbm, "p": p_hbm}
@@ -132,24 +186,32 @@
             return own[arr]
         return held[arr].at[2 * d] if col == 0 else held[arr].at[2 * d + 1, pl.ds(0, CUT)]
 
-    near_far = {1: 1, 7: 1, 2: 2, 6: 2, 3: 3, 5: 3, 4: 3}
     final = {1: "near", 7: "near", 3: "far", 5: "far", 4: "last"}
 
     def z_send(arr, col, d, hop):
         there = (d + hop) % NZ
         block = held[arr].at[2 * there + col]
         dst = block if col == 0 else held[arr].at[2 * there + 1, pl.ds(0, CUT)]
-        into = near_far[there] if col == 0 else final.get(there, "cut")
+        into = there if col == 0 else final.get(there, "cut")
         send(arr, (arr, into), piece(arr, col, d), dst, z_dev(hop))
 
     def z_first(arr, col, hops):
         for hop in hops:
             z_send(arr, col, 0, hop)
 
-    def z_relay(arr, col):
-        got((arr, 2), blocks(arr, 2)) if col == 0 else got((arr, "cut"), held[arr].at[1, pl.ds(0, 2 * CUT)])
+    def side(arr, near, far):
+        got((arr, near), blocks(arr, 1))
+        x_send(arr, near)
+        got((arr, far), blocks(arr, 1))
         for d, hop in onward[arr]:
-            z_send(arr, col, d, hop)
+            if d == far:
+                z_send(arr, 0, d, hop)
+        x_send(arr, far)
+
+    def cut_relay(arr):
+        got((arr, "cut"), held[arr].at[1, pl.ds(0, 2 * CUT)])
+        for d, hop in onward[arr]:
+            z_send(arr, 1, d, hop)
 
     def x_first(arr):
         src, dst = own[arr].at[pl.ds(0, CUT)], held[arr].at[1, pl.ds(0, CUT)]
@@ -162,11 +224,8 @@
         send(arr, (arr, into), src, held[arr].at[2 * d + 1, rest], x_dev)
 
     def x_pass(arr, *group):
-        if group[0] == 1:
-            got((arr, 1), blocks(arr, 2))
-        if group[0] == 3:
-            got((arr, 3), blocks(arr, 3))
         for d in group:
+            got((arr, d), blocks(arr, 1))
             x_send(arr, d)
 
     def second(arr):
@@ -214,62 +273,9 @@
     x_send("p", 0)
     send("chip", "chip", q_hbm, q_chip.at[1], c_dev)
     send("chip", "chip", p_hbm, p_chip.at[1], c_dev)
-    z_first("q", 0, (1, -1))
-
-    waiting(local_sems.at[0], counts_v)
-    waiting(local_sems.at[1], lines_v)
     waiting(local_sems.at[2], bank_v)
     waiting(local_sems.at[3], blocks("q", 4))
     waiting(local_sems.at[4], bank.at[0])
-    sub, lane = iota((ROWS, ROWS), 0), iota((ROWS, ROWS), 1)
-    upper = (sub <= lane).astype(F32).astype(BF)
-    lower = (lane < sub).astype(F32).astype(BF)
-    count = counts_v[...].astype(F32)
-    count_bf = count.astype(BF)
-    ends = nn(count_bf, upper) + jnp.sum(nn(lower, count_bf), axis=1, keepdims=True)
-    ends = ends - (m * GROUP).astype(F32)
-    starts = ends - count
-    inside = (ends > 0.0) & (starts < float(GROUP))
-    before = pltpu.roll(count, 1, 1)
-    before = jnp.where(lane == 0, pltpu.roll(before, 1, 0), before)
-    dd_ref[...] = jnp.where(starts <= 0.0, count, count - before)
-    starts = jnp.maximum(starts, 0.0)
-    high = jnp.floor(starts * (1.0 / ROWS))
-    lo_ref[...] = starts - high * ROWS
-    hi_ref[...] = jnp.where(inside, high, 999.0)
-    passed = jnp.sum((ends[:, ROWS - 1 :] <= 0.0).astype(F32))
-    first = jnp.minimum(passed.astype(jnp.int32), ROWS - WINDOW)
-    sub32 = iota((BLOCKS, ROWS), 0).astype(F32)
-    subf = sub.astype(F32)
-
-    def scatter(step, total):
-        lefts, rights = [], []
-        for k in range(2):
-            at = pl.ds(first + 2 * step + k, 1)
-            same = hi_ref[at, :] == sub32
-            mark = jnp.where(same, 1.0, 0.0)
-            delta = jnp.where(same, dd_ref[at, :], 0.0)
-            lefts.append(jnp.concatenate([mark, delta], axis=0).astype(BF))
-            rights.append(jnp.where(lo_ref[at, :] == subf, 1.0, 0.0).astype(BF))
-        return total + nt(jnp.concatenate(lefts, axis=1), jnp.concatenate(rights, axis=1))
-
-    marks = lax.fori_loop(0, WINDOW // 2, scatter, jnp.zeros((2 * BLOCKS, ROWS), F32))
-    low32 = (iota((BLOCKS, BLOCKS), 1) < iota((BLOCKS, BLOCKS), 0)).astype(F32).astype(BF)
-
-    def running(part):
-        part = part.astype(BF)
-        return nn(part, upper) + jnp.sum(nn(low32, part), axis=1, keepdims=True)
-
-    reqf[...] = running(marks[:BLOCKS])
-    wf[...] = 1.0 / running(marks[BLOCKS:])
-    idf[...] = lines_v[0].astype(F32)
-    shf[...] = -lines_v[1].astype(F32) * UNIT
-    chip_rows = (b, b + 1 - 2 * core)
-    for k, at in enumerate(chip_rows):
-        rows = pl.ds(k * ROWS, ROWS)
-        id_c[rows, :] = as_rows(idf[pl.ds(at, 1), :])
-        req_c[rows, :] = as_rows(reqf[pl.ds(at, 1), :])
-        sh_c[rows, :] = as_rows(shf[pl.ds(at, 1), :])
 
     def pair_row(ref, d):
         z_at = lax.rem(z + NZ - d, NZ)
@@ -307,37 +313,38 @@
         t = TEMP * nt(both(p_chip), pair(q_all, d)) + wide(sh_c)
         t_ref[d] = jnp.where(keep_pair(d), t, NEG)
 
+    pl.when(z < 2)(lambda: side("p", 7, 6))
+    pl.when(z >= 2)(lambda: side("p", 1, 2))
     second("p")
-    x_pass("p", 1, 7)
     y_first(1)
     y_first(3)
-    z_relay("p", 0)
+    z_first("q", 0, (1, -1))
+    pl.when(z < 2)(lambda: side("p", 1, 2))
+    pl.when(z >= 2)(lambda: side("p", 7, 6))
     y_relay(0)
-    x_pass("p", 2, 6)
     y_first(2)
-    z_relay("p", 1)
+    cut_relay("p")
     z_first("q", 0, (2, -2))
     x_first("q")
     x_send("q", 0)
     got("chip", q_chip)
+    pl.when(z >= 6)(requests)
     row_block(0)
+    x_pass("p", 3, 5, 4)
     row_block(1)
     row_block(7)
+    second("q")
     y_relay(1)
     y_relay(3)
-    x_pass("p", 3, 5)
-    second("q")
-    x_pass("p", 4)
     row_block(2)
     row_block(6)
+    side("q", 1, 2)
+    side("q", 7, 6)
     y_relay(2)
-    x_pass("q", 1, 7)
-    z_relay("q", 0)
-    x_pass("q", 2, 6)
     row_block(3)
     row_block(5)
-    z_relay("q", 1)
     row_block(4)
+    cut_relay("q")
 
     row_max = jnp.maximum(jnp.max(mx_ref[...], axis=1, keepdims=True), FLOOR)
     lane_sum = jnp.zeros((2 * ROWS, ROWS), F32)
@@ -422,6 +429,7 @@
     got("col", col_in)
     pgrad_out[...] = TEMP * (p_acc[:ROWS, :] + col_in[...]) - own_term * q_f
 
+    assert (len(send_at), len(arrive_at)) == (SENDS, ARRIVALS)
     for out, ref in (
         ("p", blocks("p", 15)), ("q", blocks("q", 15)), ("bank", bank.at[pl.ds(0, 31)]),
         ("lse", lse_all.at[pl.ds(0, 15)]), ("chip", q_chip), ("stat", stat_out), ("half", half_out),

time: 58.2 us -> 58 us (level)
  no operation moved by 1% of the time
where the time goes in v5:
time: 58 us; the launch traced here: 57.8 us
  Pallas kernels  53.7 us (93%)
  local copies, waits for them, and re-layouts  3.44 us (6%)
  between operations  0.65 us (1%)
    pallas_call x1, Pallas kernels, body(): pl.pallas_call(kernel, out_shape=(jax.ShapeDtypeStruct((1, ROWS), F32), j...  53.7 us
    unnamed x7, local copies, waits for them, and re-layouts  3.44 us

profile of v5, /device:TPU:1, one launch (start us, length us, event | category | flops | bytes accessed | tf_op | source)
XLA Modules:
  0.0 57.8 jit_solution(17065999180167271252)
XLA Ops:
  0.6 53.7 %retrieval.1 = (f32[1,128]{1,0:T(1,128)}, f32[128,256]{1,0:T(8,128)}, f32[128,256]{1,0:T(8,128)}) custom-call(bf16[128,256]{1,0:T(8,128)(2,1)} %q_hbm.1, bf16[128,256]{1,0:T(8,128)(2,1)} %p_hbm.1, bf16[32,256]{1,0:T(8,128)(2,1)} %items_hbm.1, s32[128,128]{1,0:T(8,128)} %bitcast.12, s32[1024,128]{1,0:T(8,128)} %bitcast.7, s32[1024,128]{1,0:T(8,128)} %bitcast.8, ...), custom_call_target="tpu_custom_call" | custom-call | tf_op jit(solution)/shard_map/retrieval/pallas_call | solution.py:486
  54.3 0.0 copy-start.1
  54.3 0.7 %copy-done.1 = f32[1,128]{1,0:T(1,128)S(1)} copy-done((f32[1,128]{1,0:T(1,128)S(1)}, f32[1,128]{1,0:T(1,128)}, u32[]{:S(2)}) %copy-start.1) | copy-done | bytes 536
  55.0 0.5 copy.15
  55.5 0.0 copy-start
  55.5 1.6 %copy.16 = f32[128,256]{1,0:T(8,128)} copy(f32[128,256]{1,0:T(8,128)} %get-tuple-element.13) | data formatting | bytes 262144
  57.1 0.0 copy-done
  57.1 0.7 %copy.17 = f32[128,256]{1,0:T(8,128)} copy(f32[128,256]{1,0:T(8,128)S(1)} %copy-done) | data formatting | bytes 262144
Async XLA Ops:
  54.3 0.7 %copy-start.1 = (f32[1,128]{1,0:T(1,128)S(1)}, f32[1,128]{1,0:T(1,128)}, u32[]{:S(2)}) copy-start(f32[1,128]{1,0:T(1,128)} %get-tuple-element.6) | copy-start | bytes 1540
  55.5 1.6 %copy-start = (f32[128,256]{1,0:T(8,128)S(1)}, f32[128,256]{1,0:T(8,128)}, u32[]{:S(2)}) copy-start(f32[128,256]{1,0:T(8,128)} %get-tuple-element.14) | copy-start | bytes 393220

commit v6 on v5

--- a/solution.py
+++ b/solution.py
@@ -318,13 +318,14 @@
     second("p")
     y_first(1)
     y_first(3)
-    z_first("q", 0, (1, -1))
+    calm = (z >= 2) & (z < 5)
+    pl.when(calm)(lambda: z_first("q", 0, (1, -1, 2, -2)))
     pl.when(z < 2)(lambda: side("p", 1, 2))
     pl.when(z >= 2)(lambda: side("p", 7, 6))
     y_relay(0)
     y_first(2)
     cut_relay("p")
-    z_first("q", 0, (2, -2))
+    pl.when(~calm)(lambda: z_first("q", 0, (1, -1, 2, -2)))
     x_first("q")
     x_send("q", 0)
     got("chip", q_chip)
@@ -436,6 +437,12 @@
         ("col", col_out),
     ):
         sent(out, ref)
+
+
+def hand_over(loss_in, qgrad_in, pgrad_in, loss_out, qgrad_out, pgrad_out):
+    loss_out[...] = loss_in[...]
+    qgrad_out[...] = qgrad_in[...]
+    pgrad_out[...] = pgrad_in[...]
 
 
 def body(queries, positives, pos_ids, pos_logq, mem_items, mem_ids, mem_logq, mem_age, counts):
@@ -501,6 +508,17 @@
         queries, positives, mem_items, lines(counts), lines(pos_ids), lines(pos_logq),
         lines(mem_ids), lines(mem_logq), lines(mem_age),
     )
+    loss, query_grad, positive_grad = pl.pallas_call(
+        hand_over,
+        out_shape=(
+            jax.ShapeDtypeStruct((1, ROWS), F32),
+            jax.ShapeDtypeStruct((ROWS, DIM), F32),
+            jax.ShapeDtypeStruct((ROWS, DIM), F32),
+        ),
+        in_specs=[vmem_spec] * 3,
+        out_specs=(vmem_spec, vmem_spec, vmem_spec),
+        name="results",
+    )(loss, query_grad, positive_grad)
     return loss.reshape(ROWS), query_grad, positive_grad
 
 

time: 58 us -> 56.7 us (0.978)
  local copies, waits for them, and re-layouts: 3.44 us -> 0 us
  Pallas kernels: 53.7 us -> 55.8 us
    unnamed x7 -> x0, local copies, waits for them, and re-layouts: 3.44 us -> none
    pallas_call x0 -> x1, Pallas kernels: none -> 1.69 us  [body(): pl.pallas_call(hand_over, out_shape=(jax.ShapeDtypeStruct((1, ROWS), F32)...]
where the time goes in v6:
time: 56.7 us; the launch traced here: 56.5 us
  Pallas kernels  55.8 us (98%)
  between operations  0.64 us (1%)
    pallas_call x1, Pallas kernels, body(): pl.pallas_call(kernel, out_shape=(jax.ShapeDtypeStruct((1, ROWS), F32), j...  54.1 us
    pallas_call x1, Pallas kernels, body(): pl.pallas_call(hand_over, out_shape=(jax.ShapeDtypeStruct((1, ROWS), F32)...  1.69 us

profile of v6, /device:TPU:1, one launch (start us, length us, event | category | flops | bytes accessed | tf_op | source)
XLA Modules:
  0.0 56.5 jit_solution(4847722839041673522)
XLA Ops:
  0.6 54.1 %retrieval.1 = (f32[1,128]{1,0:T(1,128)}, f32[128,256]{1,0:T(8,128)}, f32[128,256]{1,0:T(8,128)}) custom-call(bf16[128,256]{1,0:T(8,128)(2,1)} %q_hbm.1, bf16[128,256]{1,0:T(8,128)(2,1)} %p_hbm.1, bf16[32,256]{1,0:T(8,128)(2,1)} %items_hbm.1, s32[128,128]{1,0:T(8,128)} %bitcast.12, s32[1024,128]{1,0:T(8,128)} %bitcast.7, s32[1024,128]{1,0:T(8,128)} %bitcast.8, ...), custom_call_target="tpu_custom_call" | custom-call | tf_op jit(solution)/shard_map/retrieval/pallas_call | solution.py:493
  54.8 1.7 %results.1 = (f32[1,128]{1,0:T(1,128)}, f32[128,256]{1,0:T(8,128)}, f32[128,256]{1,0:T(8,128)}) custom-call(f32[1,128]{1,0:T(1,128)} %get-tuple-element.9.loss_in, f32[128,256]{1,0:T(8,128)} %get-tuple-element.10.qgrad_in, f32[128,256]{1,0:T(8,128)} %get-tuple-element.11.pgrad_in), custom_call_target="tpu_custom_call" | custom-call | tf_op jit(solution)/shard_map/results/pallas_call | solution.py:511

commit v7 on v6

--- a/solution.py
+++ b/solution.py
@@ -331,10 +331,10 @@
     got("chip", q_chip)
     pl.when(z >= 6)(requests)
     row_block(0)
+    second("q")
     x_pass("p", 3, 5, 4)
     row_block(1)
     row_block(7)
-    second("q")
     y_relay(1)
     y_relay(3)
     row_block(2)
@@ -344,24 +344,7 @@
     y_relay(2)
     row_block(3)
     row_block(5)
-    row_block(4)
-    cut_relay("q")
-
-    row_max = jnp.maximum(jnp.max(mx_ref[...], axis=1, keepdims=True), FLOOR)
-    lane_sum = jnp.zeros((2 * ROWS, ROWS), F32)
-    for d in range(NZ):
-        e = jnp.exp(s_ref[d] - row_max)
-        lane_sum = lane_sum + e[:, :ROWS] + e[:, ROWS:]
-        e_ref[d] = e.astype(BF)
-    row_sum = jnp.sum(lane_sum, axis=1, keepdims=True)
-    max_a, sum_a = as_row(row_max[:ROWS]), as_row(row_sum[:ROWS])
-    max_p, sum_p = as_row(row_max[ROWS:]), as_row(row_sum[ROWS:])
-    stat_out[...] = jnp.where(iota((8, ROWS), 0) == 0, max_p, sum_p)
-    send("stat", "stat", stat_out, stat_in, c_dev)
-
-    x_pass("q", 3, 5, 4)
     got("bank", bank.at[pl.ds(0, 5 * NH)])
-
     q_own = q_chip[0]
     bank_max = None
     for k in range(BANK // ROWS):
@@ -380,6 +363,20 @@
         em_ref[:, k * ROWS : (k + 1) * ROWS] = e.astype(BF)
     max_c, sum_c = as_row(max_m), as_row(jnp.sum(lane_sum, axis=1, keepdims=True))
 
+    row_block(4)
+
+    row_max = jnp.maximum(jnp.max(mx_ref[...], axis=1, keepdims=True), FLOOR)
+    lane_sum = jnp.zeros((2 * ROWS, ROWS), F32)
+    for d in range(NZ):
+        e = jnp.exp(s_ref[d] - row_max)
+        lane_sum = lane_sum + e[:, :ROWS] + e[:, ROWS:]
+        e_ref[d] = e.astype(BF)
+    row_sum = jnp.sum(lane_sum, axis=1, keepdims=True)
+    max_a, sum_a = as_row(row_max[:ROWS]), as_row(row_sum[:ROWS])
+    max_p, sum_p = as_row(row_max[ROWS:]), as_row(row_sum[ROWS:])
+    stat_out[...] = jnp.where(iota((8, ROWS), 0) == 0, max_p, sum_p)
+    send("stat", "stat", stat_out, stat_in, c_dev)
+
     got("stat", stat_in)
     max_b, sum_b = stat_in[0:1, :], stat_in[1:2, :]
     top = jnp.maximum(jnp.maximum(max_a, max_b), max_c)
@@ -392,6 +389,8 @@
                 device = on_batch(xl if col == 0 else 1 - xl, lax.rem(z + d, NZ), core)
                 send("lse", ("lse", d in (3, 4, 5)), lse_all.at[0], lse_all.at[2 * d + col], device)
 
+    cut_relay("q")
+    x_pass("q", 3, 5, 4)
     for d in range(NZ):
         part = nn(e_ref[d], pair(p_all, d))
         q_acc[...] = part if d == 0 else q_acc[...] + part

time: 56.7 us -> 56.6 us (level)
  no operation moved by 1% of the time
where the time goes in v7:
time: 56.6 us; the launch traced here: 56.4 us
  Pallas kernels  55.8 us (99%)
  between operations  0.64 us (1%)
    pallas_call x1, Pallas kernels, body(): pl.pallas_call(kernel, out_shape=(jax.ShapeDtypeStruct((1, ROWS), F32), j...  54.1 us
    pallas_call x1, Pallas kernels, body(): pl.pallas_call(hand_over, out_shape=(jax.ShapeDtypeStruct((1, ROWS), F32)...  1.69 us

profile of v7, /device:TPU:1, one launch (start us, length us, event | category | flops | bytes accessed | tf_op | source)
XLA Modules:
  0.0 56.4 jit_solution(12513990956536730004)
XLA Ops:
  0.6 54.1 %retrieval.1 = (f32[1,128]{1,0:T(1,128)}, f32[128,256]{1,0:T(8,128)}, f32[128,256]{1,0:T(8,128)}) custom-call(bf16[128,256]{1,0:T(8,128)(2,1)} %q_hbm.1, bf16[128,256]{1,0:T(8,128)(2,1)} %p_hbm.1, bf16[32,256]{1,0:T(8,128)(2,1)} %items_hbm.1, s32[128,128]{1,0:T(8,128)} %bitcast.12, s32[1024,128]{1,0:T(8,128)} %bitcast.7, s32[1024,128]{1,0:T(8,128)} %bitcast.8, ...), custom_call_target="tpu_custom_call" | custom-call | tf_op jit(solution)/shard_map/retrieval/pallas_call | solution.py:492
  54.7 1.7 %results.1 = (f32[1,128]{1,0:T(1,128)}, f32[128,256]{1,0:T(8,128)}, f32[128,256]{1,0:T(8,128)}) custom-call(f32[1,128]{1,0:T(1,128)} %get-tuple-element.9.loss_in, f32[128,256]{1,0:T(8,128)} %get-tuple-element.10.qgrad_in, f32[128,256]{1,0:T(8,128)} %get-tuple-element.11.pgrad_in), custom_call_target="tpu_custom_call" | custom-call | tf_op jit(solution)/shard_map/results/pallas_call | solution.py:510

commit v8 on v7

--- a/solution.py
+++ b/solution.py
@@ -318,16 +318,14 @@
     second("p")
     y_first(1)
     y_first(3)
-    calm = (z >= 2) & (z < 5)
-    pl.when(calm)(lambda: z_first("q", 0, (1, -1, 2, -2)))
+    z_first("q", 0, (2, -2, 1, -1))
+    x_first("q")
+    x_send("q", 0)
     pl.when(z < 2)(lambda: side("p", 1, 2))
     pl.when(z >= 2)(lambda: side("p", 7, 6))
     y_relay(0)
     y_first(2)
     cut_relay("p")
-    pl.when(~calm)(lambda: z_first("q", 0, (1, -1, 2, -2)))
-    x_first("q")
-    x_send("q", 0)
     got("chip", q_chip)
     pl.when(z >= 6)(requests)
     row_block(0)

time: 56.6 us -> 55 us (0.972)
  Pallas kernels: 55.8 us -> 54.1 us
    pallas_call x1, Pallas kernels: 54.1 us -> 52.4 us  [body(): pl.pallas_call(kernel, out_shape=(jax.ShapeDtypeStruct((1, ROWS), F32), j...]
where the time goes in v8:
time: 55 us; the launch traced here: 54.8 us
  Pallas kernels  54.1 us (98%)
  between operations  0.64 us (1%)
    pallas_call x1, Pallas kernels, body(): pl.pallas_call(kernel, out_shape=(jax.ShapeDtypeStruct((1, ROWS), F32), j...  52.4 us
    pallas_call x1, Pallas kernels, body(): pl.pallas_call(hand_over, out_shape=(jax.ShapeDtypeStruct((1, ROWS), F32)...  1.69 us

profile of v8, /device:TPU:1, one launch (start us, length us, event | category | flops | bytes accessed | tf_op | source)
XLA Modules:
  0.0 54.8 jit_solution(4870415672219972341)
XLA Ops:
  0.6 52.4 %retrieval.1 = (f32[1,128]{1,0:T(1,128)}, f32[128,256]{1,0:T(8,128)}, f32[128,256]{1,0:T(8,128)}) custom-call(bf16[128,256]{1,0:T(8,128)(2,1)} %q_hbm.1, bf16[128,256]{1,0:T(8,128)(2,1)} %p_hbm.1, bf16[32,256]{1,0:T(8,128)(2,1)} %items_hbm.1, s32[128,128]{1,0:T(8,128)} %bitcast.12, s32[1024,128]{1,0:T(8,128)} %bitcast.7, s32[1024,128]{1,0:T(8,128)} %bitcast.8, ...), custom_call_target="tpu_custom_call" | custom-call | tf_op jit(solution)/shard_map/retrieval/pallas_call | solution.py:490
  53.1 1.7 %results.1 = (f32[1,128]{1,0:T(1,128)}, f32[128,256]{1,0:T(8,128)}, f32[128,256]{1,0:T(8,128)}) custom-call(f32[1,128]{1,0:T(1,128)} %get-tuple-element.9.loss_in, f32[128,256]{1,0:T(8,128)} %get-tuple-element.10.qgrad_in, f32[128,256]{1,0:T(8,128)} %get-tuple-element.11.pgrad_in), custom_call_target="tpu_custom_call" | custom-call | tf_op jit(solution)/shard_map/results/pallas_call | solution.py:508
